TPU v7x, 32 devices: a whole 2x2x4 slice. The times are simulated.
32 devices in a mesh: groups: 1, row: 32 (over z, y, x, core), col: 1.
Axes of the slice: x: 2, y: 2, z: 4, core: 2. Of those that a mesh axis runs over, the one named last changes fastest.
Arguments:
- features_in: bfloat16 [64, 128, 128], P(None, ('groups', 'row'), 'col'), may hold values from -6 to 6
- gain_outer: float32 [8, 64], replicated, may hold values from 0.25 to 1.75
- bias_outer: float32 [8, 64], replicated, may hold values from -3 to 3
- w_narrow: bfloat16 [8, 32, 576], replicated, may hold values from -0.25 to 0.25
- gain_inner: float32 [8, 32], replicated, may hold values from 0.25 to 1.75
- bias_inner: float32 [8, 32], replicated, may hold values from -3 to 3
- w_widen: bfloat16 [8, 64, 288], replicated, may hold values from -0.375 to 0.375
Outputs:
- features_out: bfloat16 [64, 128, 128], P(None, ('groups', 'row'), 'col')
All inputs are finite; a program needn't handle non-finite values.
Results may differ from a plain program's by a relative error of at most 0.022.
Values may be sent and summed in bfloat16 or wider, within the bound.
No kernel may reach another device: no remote copies, remote signals or barrier semaphores. Data moves between devices by JAX's collectives and lax.ppermute only.
A program may use at most 64 MiB of HBM per device.

v0:
```python
import jax
import jax.numpy as jnp
from jax import lax
from jax.sharding import PartitionSpec as P


def padded_2(block, sides, width):
    for axis, dim in sides:
        count = lax.axis_size(axis)
        forward = [(i, i + 1) for i in range(count - 1)]
        backward = [(target, source) for source, target in forward]
        low = lax.ppermute(
            lax.slice_in_dim(block, block.shape[dim] - width, None, axis=dim), axis, forward
        )
        high = lax.ppermute(lax.slice_in_dim(block, 0, width, axis=dim), axis, backward)
        block = jnp.concatenate([low, block, high], axis=dim)
    return block


def dilated_taps(padded, weight, dilation, rows, cols):
    channels = padded.shape[0]
    total = None
    for vertical in range(3):
        for lateral in range(3):
            tap_index = vertical * 3 + lateral
            window = padded[
                :,
                vertical * dilation : vertical * dilation + rows,
                lateral * dilation : lateral * dilation + cols,
            ]
            weight_tap = weight[:, tap_index * channels : (tap_index + 1) * channels]
            term = jnp.einsum("oc,crw->orw", weight_tap, window, preferred_element_type=jnp.float32)
            total = term if total is None else total + term
    return total


def mirrored(stream):
    channels = stream.shape[0]
    rows = stream.shape[1]
    width = stream.shape[2]
    row_count = lax.axis_size("row")
    core_count = lax.axis_size("col")
    squares = stream.reshape(channels, rows, row_count, core_count, rows)
    outgoing = squares.transpose(3, 2, 4, 1, 0).reshape(
        core_count, row_count, rows * rows * channels
    )
    received = lax.all_to_all(
        lax.all_to_all(outgoing, "row", split_axis=1, concat_axis=1, tiled=True),
        "col",
        split_axis=0,
        concat_axis=0,
        tiled=True,
    )
    partner = (
        received.reshape(core_count, row_count, rows, rows, channels)
        .transpose(4, 2, 1, 0, 3)
        .reshape(channels, rows, width)
    )
    return ((stream.astype(jnp.float32) + partner.astype(jnp.float32)) * 0.5).astype(jnp.bfloat16)


def averaged_tiles(stream):
    strips = lax.all_to_all(stream, "col", split_axis=1, concat_axis=2, tiled=True)
    merged = mirrored(strips)
    return lax.all_to_all(merged, "col", split_axis=2, concat_axis=1, tiled=True)


def inside_mask(row_start, col_start, offset, row_count, col_count, side):
    global_rows = row_start - offset + lax.iota(jnp.int32, row_count)
    global_cols = col_start - offset + lax.iota(jnp.int32, col_count)
    rows_ok = (global_rows >= 0) & (global_rows < side)
    cols_ok = (global_cols >= 0) & (global_cols < side)
    return (rows_ok[:, None] & cols_ok[None, :])[None]


def body(features_in, gain_outer, bias_outer, w_narrow, gain_inner, bias_inner, w_widen):
    stream = features_in
    rows = stream.shape[1]
    cols = stream.shape[2]
    side = rows * lax.axis_size("row")
    rounds = gain_outer.shape[0] // 4
    row_start = lax.axis_index("row") * rows
    col_start = lax.axis_index("col") * cols
    for repeat in range(rounds):
        stream = averaged_tiles(stream)
        for within in range(4):
            block = repeat * 4 + within
            dilation = 1 + within // 2
            outer_scale = gain_outer[block][:, None, None]
            outer_shift = bias_outer[block][:, None, None]
            inner_scale = gain_inner[block][:, None, None]
            inner_shift = bias_inner[block][:, None, None]
            deep = padded_2(stream, (("row", 1), ("col", 2)), 2 * dilation)
            hidden = jax.nn.relu(deep.astype(jnp.float32) * outer_scale + outer_shift)
            hidden = jnp.where(
                inside_mask(
                    row_start,
                    col_start,
                    2 * dilation,
                    rows + 4 * dilation,
                    cols + 4 * dilation,
                    side,
                ),
                hidden,
                0.0,
            ).astype(jnp.bfloat16)
            narrow = dilated_taps(
                hidden, w_narrow[block], dilation, rows + 2 * dilation, cols + 2 * dilation
            )
            inner = jax.nn.relu(narrow * inner_scale + inner_shift)
            inner = jnp.where(
                inside_mask(
                    row_start, col_start, dilation, rows + 2 * dilation, cols + 2 * dilation, side
                ),
                inner,
                0.0,
            ).astype(jnp.bfloat16)
            widened = dilated_taps(inner, w_widen[block], dilation, rows, cols)
            stream = (stream.astype(jnp.float32) + widened).astype(jnp.bfloat16)
    return stream


def solution(mesh):
    in_specs = (P(None, ("groups", "row"), "col"), P(), P(), P(), P(), P(), P())
    out_specs = P(None, ("groups", "row"), "col")
    return jax.shard_map(body, mesh=mesh, in_specs=in_specs, out_specs=out_specs, check_vma=False)
```

profile of v0, /device:TPU:7, one launch (start us, length us, event | category | flops | bytes accessed | tf_op | source)
XLA Modules:
  0.0 155.5 jit_solution(2823055591857940647)
XLA Ops:
  0.0 1.0 copy.37
  1.2 0.6 broadcast.270
  1.8 1.0 reduce.4
  2.8 0.7 reshape.335
  3.5 6.4 %all-to-all-start = ((bf16[32,2,512]{2,1,0:T(2,128)(2,1)}), bf16[32,2,512]{2,1,0:T(2,128)(2,1)S(1)}, u32[]{:S(2)}, u32[]{:S(2)}) async-start(bf16[32,2,512]{2,1,0:T(2,128)(2,1)} %reshape.335), calls=%async_computation | async-start | bytes 131072 | tf_op jit(solution)/shard_map/all_to_all | solution.py:48
  10.0 0.6 copy-done.3
  10.7 0.7 copy-done.5
  11.4 3.7 %all-to-all-done = bf16[32,2,512]{2,1,0:T(2,128)(2,1)S(1)} async-done(((bf16[32,2,512]{2,1,0:T(2,128)(2,1)}), bf16[32,2,512]{2,1,0:T(2,128)(2,1)S(1)}, u32[]{:S(2)}, u32[]{:S(2)}) %all-to-all-start) | async-done | bytes 65568 | tf_op jit(solution)/shard_map/all_to_all | solution.py:48
  15.2 0.3 convert_reduce_fusion.1
  16.0 0.7 copy-done.2
  16.7 4.3 %collective-permute-start = (bf16[64,2,128]{2,0,1:T(8,128)(2,1)S(1)}, bf16[64,2,128]{2,0,1:T(8,128)(2,1)S(1)}, u32[]{:S(2)}, u32[]{:S(2)}) collective-permute-start(bf16[64,2,128]{2,0,1:T(8,128)(2,1)S(1)} %get-tuple-element.43), channel_id=1, source_target_pairs={{0,1},{1,2},{2,3},{3,4},{4,5},{5,6},{6,7},{7,8},{8,9},{9,10},{10,1... | collective-permute-start | bytes 98312 | tf_op jit(solution)/shard_map/ppermute | solution.py:12
  21.0 1.9 %collective-permute-start.1 = (bf16[64,2,128]{2,0,1:T(8,128)(2,1)S(1)}, bf16[64,2,128]{2,0,1:T(8,128)(2,1)S(1)}, u32[]{:S(2)}, u32[]{:S(2)}) collective-permute-start(bf16[64,2,128]{2,0,1:T(8,128)(2,1)S(1)} %get-tuple-element.44), channel_id=1, source_target_pairs={{1,0},{2,1},{3,2},{4,3},{5,4},{6,5},{7,6},{8,7},{9,8},{10,9},{11,1... | collective-permute-start | bytes 98312 | tf_op jit(solution)/shard_map/ppermute | solution.py:15
  23.0 5.1 %collective-permute-done.1 = bf16[64,2,128]{2,0,1:T(8,128)(2,1)S(1)} collective-permute-done((bf16[64,2,128]{2,0,1:T(8,128)(2,1)S(1)}, bf16[64,2,128]{2,0,1:T(8,128)(2,1)S(1)}, u32[]{:S(2)}, u32[]{:S(2)}) %collective-permute-start.1) | collective-permute-done | bytes 32800 | tf_op jit(solution)/shard_map/ppermute | solution.py:15
  28.2 0.7 collective-permute-start.2
  28.8 0.7 collective-permute-start.3
  34.1 1.9 %collective-permute-start.4 = (bf16[64,2,128]{2,0,1:T(8,128)(2,1)S(1)}, bf16[64,2,128]{2,0,1:T(8,128)(2,1)S(1)}, u32[]{:S(2)}, u32[]{:S(2)}) collective-permute-start(bf16[64,2,128]{2,0,1:T(8,128)(2,1)S(1)} %get-tuple-element.41), channel_id=1, source_target_pairs={{0,1},{1,2},{2,3},{3,4},{4,5},{5,6},{6,7},{7,8},{8,9},{9,10},{10,1... | collective-permute-start | bytes 98312 | tf_op jit(solution)/shard_map/ppermute | solution.py:12
  36.1 2.4 %collective-permute-start.5 = (bf16[64,2,128]{2,0,1:T(8,128)(2,1)S(1)}, bf16[64,2,128]{2,0,1:T(8,128)(2,1)S(1)}, u32[]{:S(2)}, u32[]{:S(2)}) collective-permute-start(bf16[64,2,128]{2,0,1:T(8,128)(2,1)S(1)} %get-tuple-element.42), channel_id=1, source_target_pairs={{1,0},{2,1},{3,2},{4,3},{5,4},{6,5},{7,6},{8,7},{9,8},{10,9},{11,1... | collective-permute-start | bytes 98312 | tf_op jit(solution)/shard_map/ppermute | solution.py:15
  38.5 4.6 %collective-permute-done.5 = bf16[64,2,128]{2,0,1:T(8,128)(2,1)S(1)} collective-permute-done((bf16[64,2,128]{2,0,1:T(8,128)(2,1)S(1)}, bf16[64,2,128]{2,0,1:T(8,128)(2,1)S(1)}, u32[]{:S(2)}, u32[]{:S(2)}) %collective-permute-start.5) | collective-permute-done | bytes 32800 | tf_op jit(solution)/shard_map/ppermute | solution.py:15
  43.2 0.7 collective-permute-start.6
  43.9 0.7 collective-permute-start.7
  49.1 1.9 %collective-permute-start.8 = (bf16[64,4,128]{2,0,1:T(8,128)(2,1)S(1)}, bf16[64,4,128]{2,0,1:T(8,128)(2,1)S(1)}, u32[]{:S(2)}, u32[]{:S(2)}) collective-permute-start(bf16[64,4,128]{2,0,1:T(8,128)(2,1)S(1)} %fusion.65), channel_id=1, source_target_pairs={{0,1},{1,2},{2,3},{3,4},{4,5},{5,6},{6,7},{7,8},{8,9},{9,10},{10,1... | collective-permute-start | bytes 196616 | tf_op jit(solution)/shard_map/ppermute | solution.py:12
  51.0 2.4 %collective-permute-start.9 = (bf16[64,4,128]{2,0,1:T(8,128)(2,1)S(1)}, bf16[64,4,128]{2,0,1:T(8,128)(2,1)S(1)}, u32[]{:S(2)}, u32[]{:S(2)}) collective-permute-start(bf16[64,4,128]{2,0,1:T(8,128)(2,1)S(1)} %fusion.65), channel_id=1, source_target_pairs={{1,0},{2,1},{3,2},{4,3},{5,4},{6,5},{7,6},{8,7},{9,8},{10,9},{11,1... | collective-permute-start | bytes 196616 | tf_op jit(solution)/shard_map/ppermute | solution.py:15
  53.5 4.9 %collective-permute-done.9 = bf16[64,4,128]{2,0,1:T(8,128)(2,1)S(1)} collective-permute-done((bf16[64,4,128]{2,0,1:T(8,128)(2,1)S(1)}, bf16[64,4,128]{2,0,1:T(8,128)(2,1)S(1)}, u32[]{:S(2)}, u32[]{:S(2)}) %collective-permute-start.9) | collective-permute-done | bytes 65568 | tf_op jit(solution)/shard_map/ppermute | solution.py:15
  58.6 0.7 collective-permute-start.10
  59.2 0.7 collective-permute-start.11
  60.1 0.3 select_convert_fusion.3
  61.4 0.3 convolution_add_fusion.28
  62.5 0.3 fusion.40
  64.8 1.9 %collective-permute-start.12 = (bf16[64,4,128]{2,0,1:T(8,128)(2,1)S(1)}, bf16[64,4,128]{2,0,1:T(8,128)(2,1)S(1)}, u32[]{:S(2)}, u32[]{:S(2)}) collective-permute-start(bf16[64,4,128]{2,0,1:T(8,128)(2,1)S(1)} %fusion.66), channel_id=1, source_target_pairs={{0,1},{1,2},{2,3},{3,4},{4,5},{5,6},{6,7},{7,8},{8,9},{9,10},{10,1... | collective-permute-start | bytes 196616 | tf_op jit(solution)/shard_map/ppermute | solution.py:12
  66.7 2.4 %collective-permute-start.13 = (bf16[64,4,128]{2,0,1:T(8,128)(2,1)S(1)}, bf16[64,4,128]{2,0,1:T(8,128)(2,1)S(1)}, u32[]{:S(2)}, u32[]{:S(2)}) collective-permute-start(bf16[64,4,128]{2,0,1:T(8,128)(2,1)S(1)} %fusion.66), channel_id=1, source_target_pairs={{1,0},{2,1},{3,2},{4,3},{5,4},{6,5},{7,6},{8,7},{9,8},{10,9},{11,1... | collective-permute-start | bytes 196616 | tf_op jit(solution)/shard_map/ppermute | solution.py:15
  69.2 5.0 %collective-permute-done.13 = bf16[64,4,128]{2,0,1:T(8,128)(2,1)S(1)} collective-permute-done((bf16[64,4,128]{2,0,1:T(8,128)(2,1)S(1)}, bf16[64,4,128]{2,0,1:T(8,128)(2,1)S(1)}, u32[]{:S(2)}, u32[]{:S(2)}) %collective-permute-start.13) | collective-permute-done | bytes 65568 | tf_op jit(solution)/shard_map/ppermute | solution.py:15
  74.3 0.7 collective-permute-start.14
  74.9 0.8 collective-permute-start.15
  75.9 0.3 select_convert_fusion.2
  77.3 0.3 convolution_add_fusion.20
  78.3 0.3 fusion.41
  81.0 1.0 reduce.5
  82.1 8.2 %all_to_all.10 = bf16[32,2,512]{2,1,0:T(2,128)(2,1)S(1)} all-to-all(bf16[32,2,512]{2,1,0:T(2,128)(2,1)S(1)} %reshape.337), channel_id=1, replica_groups=mesh['groups'=1,'row'=32,'col'=1] {'row'}, dimensions={0} | all-to-all | bytes 131072 | tf_op jit(solution)/shard_map/all_to_all | solution.py:48
  90.3 0.3 convert_reduce_fusion
  91.0 4.3 %collective-permute-start.16 = (bf16[64,2,128]{2,0,1:T(8,128)(2,1)S(1)}, bf16[64,2,128]{2,0,1:T(8,128)(2,1)S(1)}, u32[]{:S(2)}, u32[]{:S(2)}) collective-permute-start(bf16[64,2,128]{2,0,1:T(8,128)(2,1)S(1)} %get-tuple-element.39), channel_id=1, source_target_pairs={{0,1},{1,2},{2,3},{3,4},{4,5},{5,6},{6,7},{7,8},{8,9},{9,10},{10,1... | collective-permute-start | bytes 98312 | tf_op jit(solution)/shard_map/ppermute | solution.py:12
  95.3 1.9 %collective-permute-start.17 = (bf16[64,2,128]{2,0,1:T(8,128)(2,1)S(1)}, bf16[64,2,128]{2,0,1:T(8,128)(2,1)S(1)}, u32[]{:S(2)}, u32[]{:S(2)}) collective-permute-start(bf16[64,2,128]{2,0,1:T(8,128)(2,1)S(1)} %get-tuple-element.40), channel_id=1, source_target_pairs={{1,0},{2,1},{3,2},{4,3},{5,4},{6,5},{7,6},{8,7},{9,8},{10,9},{11,1... | collective-permute-start | bytes 98312 | tf_op jit(solution)/shard_map/ppermute | solution.py:15
  97.3 5.1 %collective-permute-done.17 = bf16[64,2,128]{2,0,1:T(8,128)(2,1)S(1)} collective-permute-done((bf16[64,2,128]{2,0,1:T(8,128)(2,1)S(1)}, bf16[64,2,128]{2,0,1:T(8,128)(2,1)S(1)}, u32[]{:S(2)}, u32[]{:S(2)}) %collective-permute-start.17) | collective-permute-done | bytes 32800 | tf_op jit(solution)/shard_map/ppermute | solution.py:15
  102.5 0.7 collective-permute-start.18
  103.2 0.7 collective-permute-start.19
  108.4 1.9 %collective-permute-start.20 = (bf16[64,2,128]{2,0,1:T(8,128)(2,1)S(1)}, bf16[64,2,128]{2,0,1:T(8,128)(2,1)S(1)}, u32[]{:S(2)}, u32[]{:S(2)}) collective-permute-start(bf16[64,2,128]{2,0,1:T(8,128)(2,1)S(1)} %get-tuple-element.37), channel_id=1, source_target_pairs={{0,1},{1,2},{2,3},{3,4},{4,5},{5,6},{6,7},{7,8},{8,9},{9,10},{10,1... | collective-permute-start | bytes 98312 | tf_op jit(solution)/shard_map/ppermute | solution.py:12
  110.3 2.4 %collective-permute-start.21 = (bf16[64,2,128]{2,0,1:T(8,128)(2,1)S(1)}, bf16[64,2,128]{2,0,1:T(8,128)(2,1)S(1)}, u32[]{:S(2)}, u32[]{:S(2)}) collective-permute-start(bf16[64,2,128]{2,0,1:T(8,128)(2,1)S(1)} %get-tuple-element.38), channel_id=1, source_target_pairs={{1,0},{2,1},{3,2},{4,3},{5,4},{6,5},{7,6},{8,7},{9,8},{10,9},{11,1... | collective-permute-start | bytes 98312 | tf_op jit(solution)/shard_map/ppermute | solution.py:15
  112.7 4.6 %collective-permute-done.21 = bf16[64,2,128]{2,0,1:T(8,128)(2,1)S(1)} collective-permute-done((bf16[64,2,128]{2,0,1:T(8,128)(2,1)S(1)}, bf16[64,2,128]{2,0,1:T(8,128)(2,1)S(1)}, u32[]{:S(2)}, u32[]{:S(2)}) %collective-permute-start.21) | collective-permute-done | bytes 32800 | tf_op jit(solution)/shard_map/ppermute | solution.py:15
  117.5 0.7 collective-permute-start.22
  118.1 0.7 collective-permute-start.23
  123.3 1.9 %collective-permute-start.24 = (bf16[64,4,128]{2,0,1:T(8,128)(2,1)S(1)}, bf16[64,4,128]{2,0,1:T(8,128)(2,1)S(1)}, u32[]{:S(2)}, u32[]{:S(2)}) collective-permute-start(bf16[64,4,128]{2,0,1:T(8,128)(2,1)S(1)} %fusion.69), channel_id=1, source_target_pairs={{0,1},{1,2},{2,3},{3,4},{4,5},{5,6},{6,7},{7,8},{8,9},{9,10},{10,1... | collective-permute-start | bytes 196616 | tf_op jit(solution)/shard_map/ppermute | solution.py:12
  125.2 2.4 %collective-permute-start.25 = (bf16[64,4,128]{2,0,1:T(8,128)(2,1)S(1)}, bf16[64,4,128]{2,0,1:T(8,128)(2,1)S(1)}, u32[]{:S(2)}, u32[]{:S(2)}) collective-permute-start(bf16[64,4,128]{2,0,1:T(8,128)(2,1)S(1)} %fusion.69), channel_id=1, source_target_pairs={{1,0},{2,1},{3,2},{4,3},{5,4},{6,5},{7,6},{8,7},{9,8},{10,9},{11,1... | collective-permute-start | bytes 196616 | tf_op jit(solution)/shard_map/ppermute | solution.py:15
  127.7 5.0 %collective-permute-done.25 = bf16[64,4,128]{2,0,1:T(8,128)(2,1)S(1)} collective-permute-done((bf16[64,4,128]{2,0,1:T(8,128)(2,1)S(1)}, bf16[64,4,128]{2,0,1:T(8,128)(2,1)S(1)}, u32[]{:S(2)}, u32[]{:S(2)}) %collective-permute-start.25) | collective-permute-done | bytes 65568 | tf_op jit(solution)/shard_map/ppermute | solution.py:15
  132.8 0.7 collective-permute-start.26
  133.5 0.7 collective-permute-start.27
  134.3 0.3 select_convert_fusion.1
  136.6 0.3 fusion.42
  139.0 1.9 %collective-permute-start.28 = (bf16[64,4,128]{2,0,1:T(8,128)(2,1)S(1)}, bf16[64,4,128]{2,0,1:T(8,128)(2,1)S(1)}, u32[]{:S(2)}, u32[]{:S(2)}) collective-permute-start(bf16[64,4,128]{2,0,1:T(8,128)(2,1)S(1)} %fusion.70), channel_id=1, source_target_pairs={{0,1},{1,2},{2,3},{3,4},{4,5},{5,6},{6,7},{7,8},{8,9},{9,10},{10,1... | collective-permute-start | bytes 196616 | tf_op jit(solution)/shard_map/ppermute | solution.py:12
  140.9 2.4 %collective-permute-start.29 = (bf16[64,4,128]{2,0,1:T(8,128)(2,1)S(1)}, bf16[64,4,128]{2,0,1:T(8,128)(2,1)S(1)}, u32[]{:S(2)}, u32[]{:S(2)}) collective-permute-start(bf16[64,4,128]{2,0,1:T(8,128)(2,1)S(1)} %fusion.70), channel_id=1, source_target_pairs={{1,0},{2,1},{3,2},{4,3},{5,4},{6,5},{7,6},{8,7},{9,8},{10,9},{11,1... | collective-permute-start | bytes 196616 | tf_op jit(solution)/shard_map/ppermute | solution.py:15
  143.3 5.0 %collective-permute-done.29 = bf16[64,4,128]{2,0,1:T(8,128)(2,1)S(1)} collective-permute-done((bf16[64,4,128]{2,0,1:T(8,128)(2,1)S(1)}, bf16[64,4,128]{2,0,1:T(8,128)(2,1)S(1)}, u32[]{:S(2)}, u32[]{:S(2)}) %collective-permute-start.29) | collective-permute-done | bytes 65568 | tf_op jit(solution)/shard_map/ppermute | solution.py:15
  148.4 0.7 collective-permute-start.30
  149.1 0.9 collective-permute-start.31
  150.1 0.3 select_convert_fusion
  152.5 0.3 fusion.43
  154.8 0.7 copy.55
  (234 shorter events, 36.6 us)
Async XLA Ops:
  1.1 8.8 %copy-start.1 = (bf16[8,32,576]{2,1,0:T(8,128)(2,1)S(1)}, bf16[8,32,576]{2,1,0:T(8,128)(2,1)}, u32[]{:S(2)}) copy-start(bf16[8,32,576]{2,1,0:T(8,128)(2,1)} %param.10) | copy-start | bytes 884740
  3.5 6.5 %copy-start = (bf16[8,64,288]{2,1,0:T(8,128)(2,1)S(1)}, bf16[8,64,288]{2,1,0:T(8,128)(2,1)}, u32[]{:S(2)}) copy-start(bf16[8,64,288]{2,1,0:T(8,128)(2,1)} %param.13) | copy-start | bytes 884740
  3.5 11.7 %all-to-all-start = ((bf16[32,2,512]{2,1,0:T(2,128)(2,1)}), bf16[32,2,512]{2,1,0:T(2,128)(2,1)S(1)}, u32[]{:S(2)}, u32[]{:S(2)}) async-start(bf16[32,2,512]{2,1,0:T(2,128)(2,1)} %reshape.335), calls=%async_computation | async-start | bytes 131072 | tf_op jit(solution)/shard_map/all_to_all | solution.py:48
  9.9 0.7 copy-start.3
  10.0 0.7 copy-start.4
  10.7 0.7 copy-start.5
  10.7 0.7 copy-start.6
  15.8 0.8 copy-start.2
  16.7 6.2 %collective-permute-start = (bf16[64,2,128]{2,0,1:T(8,128)(2,1)S(1)}, bf16[64,2,128]{2,0,1:T(8,128)(2,1)S(1)}, u32[]{:S(2)}, u32[]{:S(2)}) collective-permute-start(bf16[64,2,128]{2,0,1:T(8,128)(2,1)S(1)} %get-tuple-element.43), channel_id=1, source_target_pairs={{0,1},{1,2},{2,3},{3,4},{4,5},{5,6},{6,7},{7,8},{8,9},{9,10},{10,1... | collective-permute-start | bytes 98312 | tf_op jit(solution)/shard_map/ppermute | solution.py:12
  21.0 7.0 %collective-permute-start.1 = (bf16[64,2,128]{2,0,1:T(8,128)(2,1)S(1)}, bf16[64,2,128]{2,0,1:T(8,128)(2,1)S(1)}, u32[]{:S(2)}, u32[]{:S(2)}) collective-permute-start(bf16[64,2,128]{2,0,1:T(8,128)(2,1)S(1)} %get-tuple-element.44), channel_id=1, source_target_pairs={{1,0},{2,1},{3,2},{4,3},{5,4},{6,5},{7,6},{8,7},{9,8},{10,9},{11,1... | collective-permute-start | bytes 98312 | tf_op jit(solution)/shard_map/ppermute | solution.py:15
  28.2 1.5 collective-permute-start.2
  28.8 0.9 collective-permute-start.3
  34.1 4.3 %collective-permute-start.4 = (bf16[64,2,128]{2,0,1:T(8,128)(2,1)S(1)}, bf16[64,2,128]{2,0,1:T(8,128)(2,1)S(1)}, u32[]{:S(2)}, u32[]{:S(2)}) collective-permute-start(bf16[64,2,128]{2,0,1:T(8,128)(2,1)S(1)} %get-tuple-element.41), channel_id=1, source_target_pairs={{0,1},{1,2},{2,3},{3,4},{4,5},{5,6},{6,7},{7,8},{8,9},{9,10},{10,1... | collective-permute-start | bytes 98312 | tf_op jit(solution)/shard_map/ppermute | solution.py:12
  36.1 7.0 %collective-permute-start.5 = (bf16[64,2,128]{2,0,1:T(8,128)(2,1)S(1)}, bf16[64,2,128]{2,0,1:T(8,128)(2,1)S(1)}, u32[]{:S(2)}, u32[]{:S(2)}) collective-permute-start(bf16[64,2,128]{2,0,1:T(8,128)(2,1)S(1)} %get-tuple-element.42), channel_id=1, source_target_pairs={{1,0},{2,1},{3,2},{4,3},{5,4},{6,5},{7,6},{8,7},{9,8},{10,9},{11,1... | collective-permute-start | bytes 98312 | tf_op jit(solution)/shard_map/ppermute | solution.py:15
  43.2 1.5 collective-permute-start.6
  43.9 0.8 collective-permute-start.7
  49.1 4.4 %collective-permute-start.8 = (bf16[64,4,128]{2,0,1:T(8,128)(2,1)S(1)}, bf16[64,4,128]{2,0,1:T(8,128)(2,1)S(1)}, u32[]{:S(2)}, u32[]{:S(2)}) collective-permute-start(bf16[64,4,128]{2,0,1:T(8,128)(2,1)S(1)} %fusion.65), channel_id=1, source_target_pairs={{0,1},{1,2},{2,3},{3,4},{4,5},{5,6},{6,7},{7,8},{8,9},{9,10},{10,1... | collective-permute-start | bytes 196616 | tf_op jit(solution)/shard_map/ppermute | solution.py:12
  51.0 7.4 %collective-permute-start.9 = (bf16[64,4,128]{2,0,1:T(8,128)(2,1)S(1)}, bf16[64,4,128]{2,0,1:T(8,128)(2,1)S(1)}, u32[]{:S(2)}, u32[]{:S(2)}) collective-permute-start(bf16[64,4,128]{2,0,1:T(8,128)(2,1)S(1)} %fusion.65), channel_id=1, source_target_pairs={{1,0},{2,1},{3,2},{4,3},{5,4},{6,5},{7,6},{8,7},{9,8},{10,9},{11,1... | collective-permute-start | bytes 196616 | tf_op jit(solution)/shard_map/ppermute | solution.py:15
  58.6 1.5 collective-permute-start.10
  59.2 0.9 collective-permute-start.11
  64.8 4.3 %collective-permute-start.12 = (bf16[64,4,128]{2,0,1:T(8,128)(2,1)S(1)}, bf16[64,4,128]{2,0,1:T(8,128)(2,1)S(1)}, u32[]{:S(2)}, u32[]{:S(2)}) collective-permute-start(bf16[64,4,128]{2,0,1:T(8,128)(2,1)S(1)} %fusion.66), channel_id=1, source_target_pairs={{0,1},{1,2},{2,3},{3,4},{4,5},{5,6},{6,7},{7,8},{8,9},{9,10},{10,1... | collective-permute-start | bytes 196616 | tf_op jit(solution)/shard_map/ppermute | solution.py:12
  66.7 7.4 %collective-permute-start.13 = (bf16[64,4,128]{2,0,1:T(8,128)(2,1)S(1)}, bf16[64,4,128]{2,0,1:T(8,128)(2,1)S(1)}, u32[]{:S(2)}, u32[]{:S(2)}) collective-permute-start(bf16[64,4,128]{2,0,1:T(8,128)(2,1)S(1)} %fusion.66), channel_id=1, source_target_pairs={{1,0},{2,1},{3,2},{4,3},{5,4},{6,5},{7,6},{8,7},{9,8},{10,9},{11,1... | collective-permute-start | bytes 196616 | tf_op jit(solution)/shard_map/ppermute | solution.py:15
  74.3 1.7 %collective-permute-start.14 = (bf16[64,12,4]{2,0,1:T(8,128)(2,1)S(1)}, bf16[64,12,4]{2,0,1:T(8,128)(2,1)S(1)}, u32[]{:S(2)}, u32[]{:S(2)}) collective-permute-start(bf16[64,12,4]{2,0,1:T(8,128)(2,1)S(1)} %get-tuple-element.25), channel_id=1, source_target_pairs={} | collective-permute-start | bytes 18440 | tf_op jit(solution)/shard_map/ppermute | solution.py:12
  74.9 1.0 collective-permute-start.15
  91.0 6.2 %collective-permute-start.16 = (bf16[64,2,128]{2,0,1:T(8,128)(2,1)S(1)}, bf16[64,2,128]{2,0,1:T(8,128)(2,1)S(1)}, u32[]{:S(2)}, u32[]{:S(2)}) collective-permute-start(bf16[64,2,128]{2,0,1:T(8,128)(2,1)S(1)} %get-tuple-element.39), channel_id=1, source_target_pairs={{0,1},{1,2},{2,3},{3,4},{4,5},{5,6},{6,7},{7,8},{8,9},{9,10},{10,1... | collective-permute-start | bytes 98312 | tf_op jit(solution)/shard_map/ppermute | solution.py:12
  95.3 7.0 %collective-permute-start.17 = (bf16[64,2,128]{2,0,1:T(8,128)(2,1)S(1)}, bf16[64,2,128]{2,0,1:T(8,128)(2,1)S(1)}, u32[]{:S(2)}, u32[]{:S(2)}) collective-permute-start(bf16[64,2,128]{2,0,1:T(8,128)(2,1)S(1)} %get-tuple-element.40), channel_id=1, source_target_pairs={{1,0},{2,1},{3,2},{4,3},{5,4},{6,5},{7,6},{8,7},{9,8},{10,9},{11,1... | collective-permute-start | bytes 98312 | tf_op jit(solution)/shard_map/ppermute | solution.py:15
  102.5 1.5 collective-permute-start.18
  103.2 0.8 collective-permute-start.19
  108.4 4.3 %collective-permute-start.20 = (bf16[64,2,128]{2,0,1:T(8,128)(2,1)S(1)}, bf16[64,2,128]{2,0,1:T(8,128)(2,1)S(1)}, u32[]{:S(2)}, u32[]{:S(2)}) collective-permute-start(bf16[64,2,128]{2,0,1:T(8,128)(2,1)S(1)} %get-tuple-element.37), channel_id=1, source_target_pairs={{0,1},{1,2},{2,3},{3,4},{4,5},{5,6},{6,7},{7,8},{8,9},{9,10},{10,1... | collective-permute-start | bytes 98312 | tf_op jit(solution)/shard_map/ppermute | solution.py:12
  110.3 7.0 %collective-permute-start.21 = (bf16[64,2,128]{2,0,1:T(8,128)(2,1)S(1)}, bf16[64,2,128]{2,0,1:T(8,128)(2,1)S(1)}, u32[]{:S(2)}, u32[]{:S(2)}) collective-permute-start(bf16[64,2,128]{2,0,1:T(8,128)(2,1)S(1)} %get-tuple-element.38), channel_id=1, source_target_pairs={{1,0},{2,1},{3,2},{4,3},{5,4},{6,5},{7,6},{8,7},{9,8},{10,9},{11,1... | collective-permute-start | bytes 98312 | tf_op jit(solution)/shard_map/ppermute | solution.py:15
  117.5 1.5 collective-permute-start.22
  118.1 0.8 collective-permute-start.23
  123.3 4.3 %collective-permute-start.24 = (bf16[64,4,128]{2,0,1:T(8,128)(2,1)S(1)}, bf16[64,4,128]{2,0,1:T(8,128)(2,1)S(1)}, u32[]{:S(2)}, u32[]{:S(2)}) collective-permute-start(bf16[64,4,128]{2,0,1:T(8,128)(2,1)S(1)} %fusion.69), channel_id=1, source_target_pairs={{0,1},{1,2},{2,3},{3,4},{4,5},{5,6},{6,7},{7,8},{8,9},{9,10},{10,1... | collective-permute-start | bytes 196616 | tf_op jit(solution)/shard_map/ppermute | solution.py:12
  125.2 7.4 %collective-permute-start.25 = (bf16[64,4,128]{2,0,1:T(8,128)(2,1)S(1)}, bf16[64,4,128]{2,0,1:T(8,128)(2,1)S(1)}, u32[]{:S(2)}, u32[]{:S(2)}) collective-permute-start(bf16[64,4,128]{2,0,1:T(8,128)(2,1)S(1)} %fusion.69), channel_id=1, source_target_pairs={{1,0},{2,1},{3,2},{4,3},{5,4},{6,5},{7,6},{8,7},{9,8},{10,9},{11,1... | collective-permute-start | bytes 196616 | tf_op jit(solution)/shard_map/ppermute | solution.py:15
  132.8 1.5 collective-permute-start.26
  133.5 0.8 collective-permute-start.27
  139.0 4.3 %collective-permute-start.28 = (bf16[64,4,128]{2,0,1:T(8,128)(2,1)S(1)}, bf16[64,4,128]{2,0,1:T(8,128)(2,1)S(1)}, u32[]{:S(2)}, u32[]{:S(2)}) collective-permute-start(bf16[64,4,128]{2,0,1:T(8,128)(2,1)S(1)} %fusion.70), channel_id=1, source_target_pairs={{0,1},{1,2},{2,3},{3,4},{4,5},{5,6},{6,7},{7,8},{8,9},{9,10},{10,1... | collective-permute-start | bytes 196616 | tf_op jit(solution)/shard_map/ppermute | solution.py:12
  140.9 7.4 %collective-permute-start.29 = (bf16[64,4,128]{2,0,1:T(8,128)(2,1)S(1)}, bf16[64,4,128]{2,0,1:T(8,128)(2,1)S(1)}, u32[]{:S(2)}, u32[]{:S(2)}) collective-permute-start(bf16[64,4,128]{2,0,1:T(8,128)(2,1)S(1)} %fusion.70), channel_id=1, source_target_pairs={{1,0},{2,1},{3,2},{4,3},{5,4},{6,5},{7,6},{8,7},{9,8},{10,9},{11,1... | collective-permute-start | bytes 196616 | tf_op jit(solution)/shard_map/ppermute | solution.py:15
  148.4 1.7 %collective-permute-start.30 = (bf16[64,12,4]{2,0,1:T(8,128)(2,1)S(1)}, bf16[64,12,4]{2,0,1:T(8,128)(2,1)S(1)}, u32[]{:S(2)}, u32[]{:S(2)}) collective-permute-start(bf16[64,12,4]{2,0,1:T(8,128)(2,1)S(1)} %get-tuple-element.21), channel_id=1, source_target_pairs={} | collective-permute-start | bytes 18440 | tf_op jit(solution)/shard_map/ppermute | solution.py:12
  149.1 1.0 collective-permute-start.31
where the time goes:
time: 156 us; the launch traced here: 155 us
  starting transfers between devices  55.7 us (36%)
  waiting for transfers between devices  43 us (28%)
  matrix products  33.4 us (21%)
  local copies, waits for them, and re-layouts  8.35 us (5%)
  blocking collectives  8.16 us (5%)
  other arithmetic  5.54 us (4%)
    ppermute x16, waiting for transfers between devices, padded_2(): lax.ppermute(lax.slice_in_dim(block, 0, width, axis=dim), axis, backward)  39.2 us
    dot_general x144, matrix products, dilated_taps(): jnp.einsum('oc,crw->orw', weight_tap, window, preferred_element_type=jnp....  33.4 us
    ppermute x16, starting transfers between devices, padded_2(): lax.ppermute(lax.slice_in_dim(block, block.shape[dim] - width, None, axis...  25.4 us
    ppermute x16, starting transfers between devices, padded_2(): lax.ppermute(lax.slice_in_dim(block, 0, width, axis=dim), axis, backward)  24 us
    all_to_all x1, blocking collectives, mirrored(): lax.all_to_all(outgoing, 'row', split_axis=1, concat_axis=1, tiled=True)  8.16 us
    all_to_all x1, starting transfers between devices, mirrored(): lax.all_to_all(outgoing, 'row', split_axis=1, concat_axis=1, tiled=True)  6.35 us
    unnamed x28, local copies, waits for them, and re-layouts  5.39 us
    all_to_all x1, waiting for transfers between devices, mirrored(): lax.all_to_all(outgoing, 'row', split_axis=1, concat_axis=1, tiled=True)  3.74 us
  transfers between devices with their start and end apart: 33, of which 9 were waited for; matrix products, arithmetic and copies ran while one was open for 1% of the time, Pallas kernels for 0%

commit v1 on v0

v1 whole, which is shorter than its diff:
```python
import functools

import jax
import jax.numpy as jnp
from jax import lax
from jax.experimental import pallas as pl
from jax.experimental.pallas import tpu as pltpu
from jax.sharding import PartitionSpec as P

F32=jnp.float32; BF=jnp.bfloat16
PAD=8

def split(n, umax):
    k = -(-n // umax)
    return k, -(-n // k)

def net_kernel(meta, own_ref, a_ref, b_ref, wn_ref, ww_ref, go_ref, bo_ref, gi_ref, bi_ref, out_ref,
               s_ref, t_ref, h_ref, i_ref, *, R, side, halo, U):
    parity = meta[0]
    g0 = meta[1]
    W = own_ref.shape[-1]
    C = own_ref.shape[1]
    M = wn_ref.shape[2] // 3
    ext = a_ref.shape[0]
    two = own_ref.shape[0]
    base = R * parity
    off_a = jnp.where(parity == 0, 0, ext + two)
    off_b = jnp.where(parity == 0, ext + two, 0)
    lane = lax.broadcasted_iota(jnp.int32, (1, W), 1)

    def valid(y):
        g = g0 + y
        return (g >= 0) & (g < side)

    def right(h, d):
        return jnp.where(lane >= d, pltpu.roll(h, d, 1), 0)

    def left(h, d):
        return jnp.where(lane < W - d, pltpu.roll(h, W - d, 1), 0)

    def sweep(fn, a, n):
        k, u = split(n // 2, U)
        if k == 1:
            for v in range(u):
                fn(a + 2 * v)
            return
        def body(i, _):
            for v in range(u):
                fn(a + 2 * (i * u + v))
            return 0
        lax.fori_loop(0, k, body, 0)

    def hidden(t, y, go, bo):
        h = jnp.maximum(t * go + bo, 0.0)
        return jnp.where(valid(y), h, 0.0).astype(BF)

    def run_pass(ps, tb, lo, n, first):
        for j in range(4):
            d = 1 + j // 2
            gi = gi_ref[ps, j]; bi = bi_ref[ps, j]
            wn = wn_ref[ps, j]; ww = ww_ref[ps, j]
            if j < 3:
                go = go_ref[ps, j + 1]; bo = bo_ref[ps, j + 1]

            def narrow(y):
                rhs = jnp.concatenate(
                    [jnp.concatenate([h_ref[y + r + (k - 1) * d] for k in range(3)], axis=0) for r in range(2)], axis=1)
                p = jnp.dot(wn, rhs, preferred_element_type=F32)
                for r in range(2):
                    q = p[:, r * W:(r + 1) * W]
                    v = right(q[0:M], d) + q[M:2 * M] + left(q[2 * M:3 * M], d)
                    v = jnp.where(valid(y + r), jnp.maximum(v * gi + bi, 0.0), 0.0)
                    i_ref[y + r, 0:M] = right(v, d).astype(BF)
                    i_ref[y + r, M:2 * M] = v.astype(BF)
                    i_ref[y + r, 2 * M:3 * M] = left(v, d).astype(BF)

            def widen(y):
                rhs = jnp.concatenate(
                    [jnp.concatenate([i_ref[y + r + (k - 1) * d] for k in range(3)], axis=0) for r in range(2)], axis=1)
                q = jnp.dot(ww, rhs, preferred_element_type=F32)
                for r in range(2):
                    old = s_ref[y + r] if j == 0 else t_ref[tb, y + r]
                    t = old + q[:, r * W:(r + 1) * W]
                    t_ref[tb, y + r] = t
                    if j < 3:
                        h_ref[y + r] = hidden(t, y + r, go, bo)

            sweep(narrow, lo + d, n - 2 * d)
            sweep(widen, lo + 2 * d, n - 4 * d)
            lo, n = lo + 2 * d, n - 4 * d

    for i in range(ext):
        s_ref[off_a + i] = a_ref[i].astype(F32)
        s_ref[off_b + i] = b_ref[i].astype(F32)
    for i in range(two):
        s_ref[ext + i] = own_ref[i].astype(F32)

    @pl.loop(0, 2)
    def _(ps):
        go = go_ref[0, 0]; bo = bo_ref[0, 0]
        def first(y):
            for r in range(2):
                h_ref[y + r] = hidden(s_ref[y + r], y + r, go, bo)
        sweep(first, base, R + 2 * halo)
        run_pass(ps, ps, base, R + 2 * halo, True)
    h2 = halo // 2
    mid = base + h2
    go = go_ref[2, 0]; bo = bo_ref[2, 0]
    def average(y):
        for r in range(2):
            t = (t_ref[0, y + r] + t_ref[1, y + r]) * 0.5
            s_ref[y + r] = t
            h_ref[y + r] = hidden(t, y + r, go, bo)
    sweep(average, mid, R + halo)
    run_pass(2, 0, mid, R + halo, False)
    for i in range(R):
        out_ref[i] = t_ref[0, base + halo + i].astype(BF)


def net(meta, own, a, b, wn, ww, go, bo, gi, bi, *, R, side, halo, U=3):
    two, C, W = own.shape
    win = two + 2 * a.shape[0] + PAD
    M = wn.shape[2] // 3
    full = lambda: pl.BlockSpec(memory_space=pltpu.VMEM)
    return pl.pallas_call(
        functools.partial(net_kernel, R=R, side=side, halo=halo, U=U),
        out_shape=jax.ShapeDtypeStruct((R, C, W), BF),
        in_specs=[pl.BlockSpec(memory_space=pltpu.SMEM)] + [full() for _ in range(9)],
        out_specs=full(),
        scratch_shapes=[pltpu.VMEM((win, C, W), F32), pltpu.VMEM((2, win, C, W), F32),
                        pltpu.VMEM((win, C, W), BF), pltpu.VMEM((win, 3 * M, W), BF)],
        compiler_params=pltpu.CompilerParams(vmem_limit_bytes=60 * 1024 * 1024),
        name="net",
    )(meta, own, a, b, wn, ww, go, bo, gi, bi)

def prep(go, bo, wn, gi, bi, ww):
    B = wn.shape[0]; M = wn.shape[1]; C = wn.shape[2] // 9
    n = wn.reshape(B, M, 3, 3, C)
    w = ww.reshape(B, C, 3, 3, M)
    n0 = n.transpose(0, 3, 1, 2, 4).reshape(B, 3 * M, 3 * C)
    n1 = n[:4].transpose(0, 2, 1, 3, 4).reshape(4, 3 * M, 3 * C)
    w0 = ww
    w1 = w[:4].transpose(0, 1, 3, 2, 4).reshape(4, C, 9 * M)
    pk = lambda v: jnp.stack([v[:4], v[:4], v[4:]])[..., None]
    return (jnp.stack([n0[:4], n1, n0[4:]]), jnp.stack([w0[:4], w1, w0[4:]]), pk(go), pk(bo), pk(gi), pk(bi))


def send_kernel(x_ref, out_ref):
    C, R, W = x_ref.shape
    pairs = out_ref.shape[0]
    cols = W // pairs
    half = cols // 2
    x = x_ref[...].astype(F32)
    rows = lax.broadcasted_iota(jnp.int32, (W // 2, W), 0)
    lanes = lax.broadcasted_iota(jnp.int32, (W // 2, W), 1)
    for y in range(R):
        plane = x[:, y].astype(BF)
        parts = []
        for lo in range(2):
            pick = (lanes == 2 * rows + lo).astype(F32).astype(BF)
            parts.append(lax.dot_general(pick, plane, (((1,), (1,)), ((), ())), preferred_element_type=F32))
        both = jnp.concatenate(parts, axis=1).astype(BF)
        for q in range(pairs):
            out_ref[q, y * half:(y + 1) * half] = both[q * half:(q + 1) * half]


def join_kernel(meta, recv_ref, x_ref, mate_ref, out_ref):
    n, r, lanes = recv_ref.shape
    C, R, W = x_ref.shape
    half = r // R
    recv = recv_ref[...].reshape(n * r, lanes)
    row = lax.broadcasted_iota(jnp.int32, (n * r, W), 0)
    col = lax.broadcasted_iota(jnp.int32, (n * r, W), 1)
    mine = x_ref[...].astype(F32)
    mate = mate_ref[...].astype(F32)
    first = meta[0] == 0
    for p in range(half):
        pick = (row == col * half + p).astype(F32).astype(BF)
        part = lax.dot_general(recv, pick, (((0,), (0,)), ((), ())), preferred_element_type=F32)
        for lo in range(2):
            y = 2 * p + lo
            own = mine[:, y % R]
            other = mate[:, y % R]
            if y < R:
                straight = jnp.where(first, own, other)
            else:
                straight = jnp.where(first, other, own)
            out_ref[y] = ((straight + part[lo * C:(lo + 1) * C]) * 0.5).astype(BF)


def vmem_call(kernel, out_shape, args, smem=0, name=None):
    return pl.pallas_call(
        kernel,
        out_shape=out_shape,
        in_specs=[pl.BlockSpec(memory_space=pltpu.SMEM)] * smem + [pl.BlockSpec(memory_space=pltpu.VMEM)] * (len(args) - smem),
        out_specs=pl.BlockSpec(memory_space=pltpu.VMEM),
        compiler_params=pltpu.CompilerParams(vmem_limit_bytes=60 * 1024 * 1024),
        name=name,
    )(*args)


def body(features_in, gain_outer, bias_outer, w_narrow, gain_inner, bias_inner, w_widen):
    x = features_in
    C, R, part_cols = x.shape
    n = lax.axis_size("row")
    cols = lax.axis_size("col")
    if cols > 1:
        x = lax.all_gather(x, "col", axis=2, tiled=True)
    W = x.shape[2]
    side = R * n
    pairs = n // 2
    halo = 24
    ops = -(-halo // (2 * R))
    me = lax.axis_index("row")
    parity = me % 2
    meta = jnp.stack([parity, (me - parity) * R - ops * 2 * R]).astype(jnp.int32)
    weights = prep(gain_outer, bias_outer, w_narrow, gain_inner, bias_inner, w_widen)

    swap = [(i, i ^ 1) for i in range(n)]
    mate = lax.ppermute(x, "row", swap)
    sent = vmem_call(send_kernel, jax.ShapeDtypeStruct((pairs, R * R, 2 * C), BF), [x], name="send")
    sent = jnp.broadcast_to(sent[:, None], (pairs, 2) + sent.shape[1:]).reshape((n,) + sent.shape[1:])
    recv = lax.all_to_all(sent, "row", split_axis=0, concat_axis=0, tiled=True)
    own = vmem_call(join_kernel, jax.ShapeDtypeStruct((2 * R, C, W), BF), [meta, recv, x, mate], smem=1, name="join")

    got = []
    for k in range(1, ops + 1):
        hop = [(i, i + 2 * k - 1) for i in range(n) if i % 2 == 1 and i + 2 * k - 1 < n]
        hop += [(i, i - 2 * k + 1) for i in range(n) if i % 2 == 0 and i - 2 * k + 1 >= 0]
        got.append(lax.ppermute(own, "row", hop))
    up = jnp.concatenate(got, axis=0)
    down = jnp.concatenate(got[::-1], axis=0)
    side_rows = jnp.where(parity == 0, down, up)
    other_rows = lax.ppermute(side_rows, "row", swap)
    out = net(meta, own, side_rows, other_rows, *weights, R=R, side=side, halo=halo, U=13)
    out = out.transpose(1, 0, 2)
    if cols > 1:
        out = lax.dynamic_slice_in_dim(out, lax.axis_index("col") * part_cols, part_cols, axis=2)
    return out


def solution(mesh):
    in_specs = (P(None, ("groups", "row"), "col"), P(), P(), P(), P(), P(), P())
    out_specs = P(None, ("groups", "row"), "col")
    return jax.shard_map(body, mesh=mesh, in_specs=in_specs, out_specs=out_specs, check_vma=False)
```

time: 156 us -> 68.7 us (0.44)
  starting transfers between devices: 55.7 us -> 17 us
  waiting for transfers between devices: 43 us -> 6.32 us
  matrix products: 33.4 us -> 0 us
  Pallas kernels: 0 us -> 26.7 us
  blocking collectives: 8.16 us -> 0 us
  local copies, waits for them, and re-layouts: 8.35 us -> 15.3 us
  other arithmetic: 5.54 us -> 2.67 us
    ppermute x32 -> x5, starting transfers between devices: 49.4 us -> 11.2 us  [the longest x3 10.4 us: body(): got.append(lax.ppermute(own, 'row', hop))]
    ppermute x32 -> x5, waiting for transfers between devices: 39.3 us -> 5.02 us  [the longest x3 5.01 us: body(): got.append(lax.ppermute(own, 'row', hop))]
    dot_general x144 -> x0, matrix products: 33.4 us -> none  [dilated_taps(): jnp.einsum('oc,crw->orw', weight_tap, window, preferred_element_type=jnp....]
    pallas_call x0 -> x3, Pallas kernels: none -> 26.7 us  [the longest x1 22.7 us: net(): pl.pallas_call(functools.partial(net_kernel, R=R, side=side, halo=halo, U...]
    all_to_all x1 -> x0, blocking collectives: 8.16 us -> none  [mirrored(): lax.all_to_all(outgoing, 'row', split_axis=1, concat_axis=1, tiled=True)]
    broadcast_in_dim x0 -> x5, local copies, waits for them, and re-layouts: none -> 5.13 us  [the longest x4 3.63 us: prep(): pk = lambda v: jnp.stack([v[:4], v[:4], v[4:]])[..., None]]
    convert_element_type x12 -> x0, other arithmetic: 3.04 us -> none  [the longest x8 2.3 us: body(): hidden = jnp.where(inside_mask(row_start, col_start, 2 * dilation, rows +...]
    another operation x0 -> x3, other arithmetic: none -> 2.58 us  [the longest x1 0.96 us: prep(): jnp.stack([n0[:4], n1, n0[4:]])]
  transfers between devices with their start and end apart: 33 -> 6, of which waited for: 9 -> 3; matrix products, arithmetic and copies ran while one was open for 1% -> 15% of each run, Pallas kernels for 0% -> 0%
where the time goes in v1:
time: 68.7 us; the launch traced here: 68.1 us
  Pallas kernels  26.7 us (39%)
  starting transfers between devices  17 us (25%)
  local copies, waits for them, and re-layouts  15.3 us (22%)
  waiting for transfers between devices  6.32 us (9%)
  other arithmetic  2.67 us (4%)
    pallas_call x1, Pallas kernels, net(): pl.pallas_call(functools.partial(net_kernel, R=R, side=side, halo=halo, U...  22.7 us
    ppermute x3, starting transfers between devices, body(): got.append(lax.ppermute(own, 'row', hop))  10.4 us
    all_to_all x1, starting transfers between devices, body(): recv = lax.all_to_all(sent, 'row', split_axis=0, concat_axis=0, tiled=True)  5.79 us
    unnamed x20, local copies, waits for them, and re-layouts  5.2 us
    ppermute x3, waiting for transfers between devices, body(): got.append(lax.ppermute(own, 'row', hop))  5.01 us
    pallas_call x2, Pallas kernels, vmem_call(): pl.pallas_call(kernel, out_shape=out_shape, in_specs=[pl.BlockSpec(memory...  3.96 us
    broadcast_in_dim x4, local copies, waits for them, and re-layouts, prep(): pk = lambda v: jnp.stack([v[:4], v[:4], v[4:]])[..., None]  3.63 us
    transpose x1, local copies, waits for them, and re-layouts, body(): out = out.transpose(1, 0, 2)  1.52 us
  transfers between devices with their start and end apart: 6, of which 3 were waited for; matrix products, arithmetic and copies ran while one was open for 15% of the time, Pallas kernels for 0%

profile of v1, /device:TPU:7, one launch (start us, length us, event | category | flops | bytes accessed | tf_op | source)
XLA Modules:
  0.0 68.1 jit_solution(16234688706317355580)
XLA Ops:
  0.0 0.0 copy-start.3
  0.0 0.7 collective-permute-start
  0.7 1.7 %send.1 = bf16[16,16,128]{2,1,0:T(8,128)(2,1)} custom-call(bf16[64,4,128]{2,1,0:T(4,128)(2,1)} %x_ref.3), custom_call_target="tpu_custom_call" | custom-call | tf_op jit(solution)/shard_map/send/pallas_call | solution.py:192
  2.4 1.5 %broadcast_in_dim.18 = bf16[16,2,16,128]{3,2,1,0:T(8,128)(2,1)} broadcast(bf16[16,16,128]{2,1,0:T(8,128)(2,1)} %send.1), dimensions={0,2,3} | broadcast | bytes 196608 | tf_op jit(solution)/shard_map/broadcast_in_dim | solution.py:222
  3.9 5.8 %all-to-all-start = ((bf16[32,16,128]{2,1,0:T(8,128)(2,1)}), bf16[32,16,128]{2,1,0:T(8,128)(2,1)S(1)}, u32[]{:S(2)}, u32[]{:S(2)}) async-start(bf16[32,16,128]{2,1,0:T(8,128)(2,1)} %bitcast.2), calls=%async_computation | async-start | bytes 262144 | tf_op jit(solution)/shard_map/all_to_all | solution.py:223
  9.7 0.0 copy-done.3
  9.7 0.0 copy-start.1
  9.8 0.1 slice_bitcast_fusion.9
  9.8 0.9 %copy-done.1 = bf16[8,32,576]{2,1,0:T(8,128)(2,1)S(1)} copy-done((bf16[8,32,576]{2,1,0:T(8,128)(2,1)S(1)}, bf16[8,32,576]{2,1,0:T(8,128)(2,1)}, u32[]{:S(2)}) %copy-start.1) | copy-done | bytes 294936
  10.7 0.4 reshape.16
  11.2 0.0 copy-start.6
  11.2 0.3 fusion.3
  11.5 0.4 copy-done.6
  11.9 0.0 copy-start.7
  11.9 0.7 copy-done.7
  12.5 0.0 copy-start.8
  12.6 0.7 copy-done.8
  13.2 0.0 copy-start.9
  13.2 0.7 copy-done.9
  13.9 0.7 pad_add_fusion.meta
  14.6 0.0 collective-permute-done.mate_ref
  14.6 0.0 copy-start.5
  14.6 1.3 %all-to-all-done.recv_ref = bf16[32,16,128]{2,1,0:T(8,128)(2,1)S(1)} async-done(((bf16[32,16,128]{2,1,0:T(8,128)(2,1)}), bf16[32,16,128]{2,1,0:T(8,128)(2,1)S(1)}, u32[]{:S(2)}, u32[]{:S(2)}) %all-to-all-start) | async-done | bytes 131104 | tf_op jit(solution)/shard_map/all_to_all | solution.py:223
  15.9 0.0 copy-done.5
  15.9 0.0 copy-start.2
  15.9 0.6 copy-done.2
  16.5 2.2 %join.1.own_ref = bf16[8,64,128]{2,1,0:T(8,128)(2,1)} custom-call(s32[2]{0:T(128)} %pad_add_fusion.meta, bf16[32,16,128]{2,1,0:T(8,128)(2,1)} %copy-done.2, bf16[64,4,128]{2,1,0:T(4,128)(2,1)} %x_ref.3, bf16[64,4,128]{2,1,0:T(4,128)(2,1)} %copy-done.5), custom_call_target="tpu_custom_call" | custom-call | tf_op jit(solution)/shard_map/join/pallas_call | solution.py:192
  18.7 3.5 %collective-permute-start.1 = (bf16[8,64,128]{2,1,0:T(8,128)(2,1)}, bf16[8,64,128]{2,1,0:T(8,128)(2,1)S(1)}, u32[]{:S(2)}, u32[]{:S(2)}) collective-permute-start(bf16[8,64,128]{2,1,0:T(8,128)(2,1)} %join.1.own_ref), channel_id=1, source_target_pairs={{1,6},{3,8},{5,10},{7,12},{9,14},{11,16},{13,18},{15,20},{17,22},{... | collective-permute-start | bytes 393224 | tf_op jit(solution)/shard_map/ppermute | solution.py:230
  22.2 3.7 %collective-permute-start.2 = (bf16[8,64,128]{2,1,0:T(8,128)(2,1)}, bf16[8,64,128]{2,1,0:T(8,128)(2,1)S(1)}, u32[]{:S(2)}, u32[]{:S(2)}) collective-permute-start(bf16[8,64,128]{2,1,0:T(8,128)(2,1)} %join.1.own_ref), channel_id=1, source_target_pairs={{1,4},{3,6},{5,8},{7,10},{9,12},{11,14},{13,16},{15,18},{17,20},{1... | collective-permute-start | bytes 393224 | tf_op jit(solution)/shard_map/ppermute | solution.py:230
  26.0 3.2 %collective-permute-start.3 = (bf16[8,64,128]{2,1,0:T(8,128)(2,1)}, bf16[8,64,128]{2,1,0:T(8,128)(2,1)S(1)}, u32[]{:S(2)}, u32[]{:S(2)}) collective-permute-start(bf16[8,64,128]{2,1,0:T(8,128)(2,1)} %join.1.own_ref), channel_id=1, source_target_pairs={{1,2},{3,4},{5,6},{7,8},{9,10},{11,12},{13,14},{15,16},{17,18},{19... | collective-permute-start | bytes 393224 | tf_op jit(solution)/shard_map/ppermute | solution.py:230
  29.2 0.0 collective-permute-done.1
  29.2 0.5 collective-permute-done.2
  29.7 4.5 %collective-permute-done.3 = bf16[8,64,128]{2,1,0:T(8,128)(2,1)S(1)} collective-permute-done((bf16[8,64,128]{2,1,0:T(8,128)(2,1)}, bf16[8,64,128]{2,1,0:T(8,128)(2,1)S(1)}, u32[]{:S(2)}, u32[]{:S(2)}) %collective-permute-start.3) | collective-permute-done | bytes 131104 | tf_op jit(solution)/shard_map/ppermute | solution.py:230
  34.2 0.1 fusion.1.a_ref
  34.3 0.0 copy-start
  34.3 0.1 collective-permute-start.4
  34.4 0.2 copy.15
  34.6 0.4 copy-done
  35.1 0.2 copy.17
  35.3 0.2 copy.12
  35.5 0.2 stack.70
  35.7 0.2 copy.14
  36.0 0.0 slice-start
  36.0 0.2 stack.71
  36.2 0.7 slice-done
  36.9 0.2 slice.54
  37.1 0.2 copy.13
  37.3 0.2 stack_reshape.6
  37.5 1.0 %copy.18.go_ref = f32[3,4,64,1]{3,2,1,0:T(8,128)} copy(f32[3,4,64,1]{2,1,0,3:T(4,128)S(1)} %maximum_bitcast_fusion) | data formatting | bytes 6144 | tf_op jit(solution)/shard_map/broadcast_in_dim | solution.py:144
  38.5 1.0 %copy.19.bo_ref = f32[3,4,64,1]{3,2,1,0:T(8,128)} copy(f32[3,4,64,1]{2,1,0,3:T(4,128)S(1)} %maximum_bitcast_fusion.1) | data formatting | bytes 6144 | tf_op jit(solution)/shard_map/broadcast_in_dim | solution.py:144
  39.5 0.8 %copy.20.gi_ref = f32[3,4,32,1]{3,2,1,0:T(8,128)} copy(f32[3,4,32,1]{2,1,0,3:T(4,128)S(1)} %maximum_bitcast_fusion.2) | data formatting | bytes 3072 | tf_op jit(solution)/shard_map/broadcast_in_dim | solution.py:144
  40.3 0.8 %copy.21.bi_ref = f32[3,4,32,1]{3,2,1,0:T(8,128)} copy(f32[3,4,32,1]{2,1,0,3:T(4,128)S(1)} %maximum_bitcast_fusion.3) | data formatting | bytes 3072 | tf_op jit(solution)/shard_map/broadcast_in_dim | solution.py:144
  41.2 1.0 %pad_maximum_fusion.1.ww_ref = bf16[3,4,64,288]{3,2,1,0:T(8,128)(2,1)} fusion(bf16[1,4,64,288]{3,2,1,0:T(8,128)(2,1)S(1)} %get-tuple-element.8, bf16[1,4,64,288]{3,2,1,0:T(8,128)(2,1)S(1)} %copy.17, bf16[1,4,64,288]{3,2,1,0:T(8,128)(2,1)S(1)} %get-tuple-element.7), kind=kLoop, calls=%fused_computation.1 | loop fusion | flops 442368 | bytes 884736 | tf_op jit(solution)/shard_map/stack | solution.py:145
  42.1 1.0 %pad_maximum_fusion.wn_ref = bf16[3,4,96,192]{3,2,1,0:T(8,128)(2,1)} fusion(bf16[1,4,96,192]{3,2,1,0:T(8,128)(2,1)S(1)} %stack.71, bf16[1,4,96,192]{3,2,1,0:T(8,128)(2,1)S(1)} %stack_reshape.6, bf16[1,4,96,192]{3,2,1,0:T(8,128)(2,1)S(1)} %stack.70), kind=kLoop, calls=%fused_computation | loop fusion | flops 442368 | bytes 884736 | tf_op jit(solution)/shard_map/stack | solution.py:145
  43.1 0.0 collective-permute-done.4.b_ref
  43.1 0.0 copy-start.4
  43.1 0.8 %copy-done.4 = bf16[24,64,128]{2,1,0:T(8,128)(2,1)} copy-done((bf16[24,64,128]{2,1,0:T(8,128)(2,1)}, bf16[24,64,128]{2,1,0:T(8,128)(2,1)S(1)}, u32[]{:S(2)}) %copy-start.4) | copy-done | bytes 393240
  43.9 22.7 %net.1 = bf16[4,64,128]{2,1,0:T(8,128)(2,1)} custom-call(s32[2]{0:T(128)} %pad_add_fusion.meta, bf16[8,64,128]{2,1,0:T(8,128)(2,1)} %join.1.own_ref, bf16[24,64,128]{2,1,0:T(8,128)(2,1)} %copy-done, bf16[24,64,128]{2,1,0:T(8,128)(2,1)} %copy-done.4, bf16[3,4,96,192]{3,2,1,0:T(8,128)(2,1)} %pad_maximum_fusion.wn_ref, ...), custom_call_target="tpu_custom_call" | custom-call | tf_op jit(solution)/shard_map/net/pallas_call | solution.py:125
  66.6 1.5 %copy.22 = bf16[64,4,128]{2,1,0:T(4,128)(2,1)} copy(bf16[64,4,128]{2,0,1:T(8,128)(2,1)} %bitcast.42) | data formatting | bytes 131072 | tf_op jit(solution)/shard_map/transpose | solution.py:236
  (9 shorter events, 0.1 us)
Async XLA Ops:
  0.0 9.7 %copy-start.3 = (bf16[8,64,288]{2,1,0:T(8,128)(2,1)S(1)}, bf16[8,64,288]{2,1,0:T(8,128)(2,1)}, u32[]{:S(2)}) copy-start(bf16[8,64,288]{2,1,0:T(8,128)(2,1)} %param.13) | copy-start | bytes 884740
  0.0 14.6 %collective-permute-start = (bf16[64,4,128]{2,1,0:T(4,128)(2,1)}, bf16[64,4,128]{2,1,0:T(4,128)(2,1)S(1)}, u32[]{:S(2)}, u32[]{:S(2)}) collective-permute-start(bf16[64,4,128]{2,1,0:T(4,128)(2,1)} %x_ref.3), channel_id=1, source_target_pairs={{0,1},{1,0},{2,3},{3,2},{4,5},{5,4},{6,7},{7,6},{8,9},{9,8},{10,11... | collective-permute-start | bytes 196616 | tf_op jit(solution)/shard_map/ppermute | solution.py:220
  3.9 12.0 %all-to-all-start = ((bf16[32,16,128]{2,1,0:T(8,128)(2,1)}), bf16[32,16,128]{2,1,0:T(8,128)(2,1)S(1)}, u32[]{:S(2)}, u32[]{:S(2)}) async-start(bf16[32,16,128]{2,1,0:T(8,128)(2,1)} %bitcast.2), calls=%async_computation | async-start | bytes 262144 | tf_op jit(solution)/shard_map/all_to_all | solution.py:223
  9.7 1.0 %copy-start.1 = (bf16[8,32,576]{2,1,0:T(8,128)(2,1)S(1)}, bf16[8,32,576]{2,1,0:T(8,128)(2,1)}, u32[]{:S(2)}) copy-start(bf16[8,32,576]{2,1,0:T(8,128)(2,1)} %param.10) | copy-start | bytes 884740
  11.2 0.7 %copy-start.6 = (f32[8,64]{1,0:T(8,128)S(1)}, f32[8,64]{1,0:T(8,128)}, u32[]{:S(2)}) copy-start(f32[8,64]{1,0:T(8,128)} %param.8) | copy-start | bytes 6148
  11.9 0.7 %copy-start.7 = (f32[8,64]{1,0:T(8,128)S(1)}, f32[8,64]{1,0:T(8,128)}, u32[]{:S(2)}) copy-start(f32[8,64]{1,0:T(8,128)} %param.9) | copy-start | bytes 6148
  12.5 0.7 %copy-start.8 = (f32[8,32]{1,0:T(8,128)S(1)}, f32[8,32]{1,0:T(8,128)}, u32[]{:S(2)}) copy-start(f32[8,32]{1,0:T(8,128)} %param.11) | copy-start | bytes 3076
  13.2 0.7 %copy-start.9 = (f32[8,32]{1,0:T(8,128)S(1)}, f32[8,32]{1,0:T(8,128)}, u32[]{:S(2)}) copy-start(f32[8,32]{1,0:T(8,128)} %param.12) | copy-start | bytes 3076
  14.6 1.3 %copy-start.5 = (bf16[64,4,128]{2,1,0:T(4,128)(2,1)}, bf16[64,4,128]{2,1,0:T(4,128)(2,1)S(1)}, u32[]{:S(2)}) copy-start(bf16[64,4,128]{2,1,0:T(4,128)(2,1)S(1)} %collective-permute-done.mate_ref) | copy-start | bytes 196612
  15.9 0.6 copy-start.2
  18.7 10.5 %collective-permute-start.1 = (bf16[8,64,128]{2,1,0:T(8,128)(2,1)}, bf16[8,64,128]{2,1,0:T(8,128)(2,1)S(1)}, u32[]{:S(2)}, u32[]{:S(2)}) collective-permute-start(bf16[8,64,128]{2,1,0:T(8,128)(2,1)} %join.1.own_ref), channel_id=1, source_target_pairs={{1,6},{3,8},{5,10},{7,12},{9,14},{11,16},{13,18},{15,20},{17,22},{... | collective-permute-start | bytes 393224 | tf_op jit(solution)/shard_map/ppermute | solution.py:230
  22.2 7.5 %collective-permute-start.2 = (bf16[8,64,128]{2,1,0:T(8,128)(2,1)}, bf16[8,64,128]{2,1,0:T(8,128)(2,1)S(1)}, u32[]{:S(2)}, u32[]{:S(2)}) collective-permute-start(bf16[8,64,128]{2,1,0:T(8,128)(2,1)} %join.1.own_ref), channel_id=1, source_target_pairs={{1,4},{3,6},{5,8},{7,10},{9,12},{11,14},{13,16},{15,18},{17,20},{1... | collective-permute-start | bytes 393224 | tf_op jit(solution)/shard_map/ppermute | solution.py:230
  26.0 8.3 %collective-permute-start.3 = (bf16[8,64,128]{2,1,0:T(8,128)(2,1)}, bf16[8,64,128]{2,1,0:T(8,128)(2,1)S(1)}, u32[]{:S(2)}, u32[]{:S(2)}) collective-permute-start(bf16[8,64,128]{2,1,0:T(8,128)(2,1)} %join.1.own_ref), channel_id=1, source_target_pairs={{1,2},{3,4},{5,6},{7,8},{9,10},{11,12},{13,14},{15,16},{17,18},{19... | collective-permute-start | bytes 393224 | tf_op jit(solution)/shard_map/ppermute | solution.py:230
  34.3 0.7 %copy-start = (bf16[24,64,128]{2,1,0:T(8,128)(2,1)}, bf16[24,64,128]{2,1,0:T(8,128)(2,1)S(1)}, u32[]{:S(2)}) copy-start(bf16[24,64,128]{2,1,0:T(8,128)(2,1)S(1)} %fusion.1.a_ref) | copy-start | bytes 1179652
  34.3 8.8 %collective-permute-start.4 = (bf16[24,64,128]{2,1,0:T(8,128)(2,1)S(1)}, bf16[24,64,128]{2,1,0:T(8,128)(2,1)S(1)}, u32[]{:S(2)}, u32[]{:S(2)}) collective-permute-start(bf16[24,64,128]{2,1,0:T(8,128)(2,1)S(1)} %fusion.1.a_ref), channel_id=1, source_target_pairs={{0,1},{1,0},{2,3},{3,2},{4,5},{5,4},{6,7},{7,6},{8,9},{9,8},{10,11... | collective-permute-start | bytes 1179656 | tf_op jit(solution)/shard_map/ppermute | solution.py:234
  36.0 0.9 %slice-start = ((bf16[8,32,576]{2,1,0:T(8,128)(2,1)}), bf16[4,32,576]{2,1,0:T(8,128)(2,1)S(1)}, s32[]{:S(2)}) async-start(bf16[8,32,576]{2,1,0:T(8,128)(2,1)} %param.10), calls=%async_computation.1 | async-start | bytes 327680 | tf_op jit(solution)/shard_map/slice | solution.py:141
  43.1 0.8 %copy-start.4 = (bf16[24,64,128]{2,1,0:T(8,128)(2,1)}, bf16[24,64,128]{2,1,0:T(8,128)(2,1)S(1)}, u32[]{:S(2)}) copy-start(bf16[24,64,128]{2,1,0:T(8,128)(2,1)S(1)} %collective-permute-done.4.b_ref) | copy-start | bytes 1179652

commit v2 on v1

v2 whole, which is shorter than its diff:
```python
import functools

import jax
import jax.numpy as jnp
from jax import lax
from jax.experimental import pallas as pl
from jax.experimental.pallas import tpu as pltpu
from jax.sharding import PartitionSpec as P

F32=jnp.float32; BF=jnp.bfloat16
LAG=6


def emission(n, lag):
    events = []
    start = 0
    for j in range(4):
        d = 1 + j // 2
        na, nb = n // 2 - d, n // 2 - 2 * d
        for p in range(na):
            events.append((start + p, 1, j, p, "narrow"))
        for q in range(nb):
            events.append((start + q + d + lag, 0, j, q, "widen"))
        nd = 1 + (j + 1) // 2
        start = max(start + na, start + d + lag + nd + 1)
        n -= 4 * d
    return [(j, p, kind) for _, _, j, p, kind in sorted(events, key=lambda e: e[:2])]


def net_kernel(own_ref, a_ref, b_ref, wn_ref, ww_ref, wt_ref, po_ref, pi_ref, out_ref,
               s_ref, t_ref, h_ref, i_ref, *, R, side, halo, lag):
    me = lax.axis_index("row")
    parity = lax.rem(me, 2)
    g0 = (me - parity) * R - a_ref.shape[0]
    W = own_ref.shape[-1]
    C = own_ref.shape[1]
    M = wn_ref.shape[1] // 3
    ext = a_ref.shape[0]
    two = own_ref.shape[0]
    base = R
    shift = R - R * parity
    lane = lax.broadcasted_iota(jnp.int32, (1, W), 1)

    def valid(y):
        g = g0 + y - shift
        return (g >= 0) & (g < side)

    def right(h, d):
        return jnp.where(lane >= d, pltpu.roll(h, d, 1), 0)

    def left(h, d):
        return jnp.where(lane < W - d, pltpu.roll(h, W - d, 1), 0)

    def hidden(t, y, k):
        h = jnp.maximum(t * po_ref[k, 0:C] + po_ref[k, C:2 * C], 0.0)
        return jnp.where(valid(y), h, 0.0).astype(BF)

    def run_pass(tb, lo, n, narrow_row, widen_of, block0):
        los = []
        at = lo
        for j in range(4):
            los.append(at)
            at = at + 2 * (1 + j // 2)

        def narrow(j, y):
            d = 1 + j // 2
            rhs = jnp.concatenate(
                [jnp.concatenate([h_ref[y + r + (k - 1) * d] for k in range(3)], axis=0) for r in range(2)], axis=1)
            p = jnp.dot(wn_ref[narrow_row + j], rhs, preferred_element_type=F32)
            gi = pi_ref[block0 + j, 0:M]
            bi = pi_ref[block0 + j, M:2 * M]
            for r in range(2):
                q = p[:, r * W:(r + 1) * W]
                v = right(q[0:M], d) + q[M:2 * M] + left(q[2 * M:3 * M], d)
                v = jnp.where(valid(y + r), jnp.maximum(v * gi + bi, 0.0), 0.0)
                i_ref[y + r, 0:M] = right(v, d).astype(BF)
                i_ref[y + r, M:2 * M] = v.astype(BF)
                i_ref[y + r, 2 * M:3 * M] = left(v, d).astype(BF)

        def widen(j, y):
            d = 1 + j // 2
            rhs = jnp.concatenate(
                [jnp.concatenate([i_ref[y + r + (k - 1) * d] for k in range(3)], axis=0) for r in range(2)], axis=1)
            q = jnp.dot(widen_of(j), rhs, preferred_element_type=F32)
            for r in range(2):
                old = s_ref[y + r] if j == 0 else t_ref[tb, y + r]
                t = old + q[:, r * W:(r + 1) * W]
                t_ref[tb, y + r] = t
                if j < 3:
                    h_ref[y + r] = hidden(t, y + r, block0 + j + 1)

        for j, p, kind in emission(n, lag):
            d = 1 + j // 2
            if kind == "narrow":
                narrow(j, los[j] + d + 2 * p)
            else:
                widen(j, los[j] + 2 * d + 2 * p)

    pairs = ext // two
    for k in range(pairs):
        at_a = jnp.where(parity == 0, pairs - 1 - k, pairs + 1 + k) * two
        at_b = jnp.where(parity == 0, pairs + 1 + k, pairs - 1 - k) * two
        for i in range(two):
            s_ref[at_a + shift + i] = a_ref[k * two + i].astype(F32)
            s_ref[at_b + shift + i] = b_ref[k * two + i].astype(F32)
    for i in range(two):
        s_ref[ext + shift + i] = own_ref[i].astype(F32)

    @pl.loop(0, 2)
    def _(ps):
        for i in range(R + 2 * halo):
            h_ref[base + i] = hidden(s_ref[base + i], base + i, 0)
        run_pass(ps, base, R + 2 * halo, 4 * ps, lambda j: wt_ref[4 * ps + j], 0)
    mid = base + halo // 2
    for i in range(R + halo):
        t = (t_ref[0, mid + i] + t_ref[1, mid + i]) * 0.5
        s_ref[mid + i] = t
        h_ref[mid + i] = hidden(t, mid + i, 4)
    run_pass(0, mid, R + halo, 8, lambda j: ww_ref[4 + j], 4)
    for i in range(R):
        out_ref[:, i] = t_ref[0, base + halo + i].astype(BF)


def net(own, a, b, wn, ww, wt, po, pi, *, R, side, halo, U=LAG):
    two, C, W = own.shape
    win = two + 2 * a.shape[0] + R
    M = wn.shape[1] // 3
    full = lambda: pl.BlockSpec(memory_space=pltpu.VMEM)
    return pl.pallas_call(
        functools.partial(net_kernel, R=R, side=side, halo=halo, lag=U),
        out_shape=jax.ShapeDtypeStruct((C, R, W), BF),
        in_specs=[full() for _ in range(8)],
        out_specs=full(),
        scratch_shapes=[pltpu.VMEM((win, C, W), F32), pltpu.VMEM((2, win, C, W), F32),
                        pltpu.VMEM((win, C, W), BF), pltpu.VMEM((win, 3 * M, W), BF)],
        compiler_params=pltpu.CompilerParams(vmem_limit_bytes=min(15 * W // 128, 60) * 1024 * 1024),
        name="net",
    )(own, a, b, wn, ww, wt, po, pi)


def prep_kernel(go_ref, bo_ref, wn_ref, gi_ref, bi_ref, ww_ref, n_ref, t_ref, po_ref, pi_ref):
    B, C = go_ref.shape
    M = gi_ref.shape[1]
    W = po_ref.shape[2]
    half = B // 2
    for k in range(B):
        w = wn_ref[k].astype(F32)
        row = k if k < half else k + half
        for kx in range(3):
            n_ref[row, kx * M:(kx + 1) * M] = jnp.concatenate(
                [w[:, (3 * ky + kx) * C:(3 * ky + kx + 1) * C] for ky in range(3)], axis=1).astype(BF)
            if k < half:
                n_ref[k + half, kx * M:(kx + 1) * M] = w[:, 3 * kx * C:3 * (kx + 1) * C].astype(BF)
        if k < half:
            v = ww_ref[k]
            t_ref[k] = v
            v = v.astype(F32)
            t_ref[k + half] = jnp.concatenate(
                [v[:, (3 * kx + ky) * M:(3 * kx + ky + 1) * M] for ky in range(3) for kx in range(3)], axis=1).astype(BF)
    outer = jnp.concatenate([go_ref[...], bo_ref[...]], axis=1).T
    inner = jnp.concatenate([gi_ref[...], bi_ref[...]], axis=1).T
    for k in range(B):
        po_ref[k] = jnp.broadcast_to(outer[:, k:k + 1], (2 * C, W))
        pi_ref[k] = jnp.broadcast_to(inner[:, k:k + 1], (2 * M, W))


def prep(go, bo, wn, gi, bi, ww, W=128):
    B, C = go.shape
    M = gi.shape[1]
    out = (jax.ShapeDtypeStruct((B + B // 2, 3 * M, 3 * C), BF), jax.ShapeDtypeStruct((B, C, 9 * M), BF),
           jax.ShapeDtypeStruct((B, 2 * C, W), F32), jax.ShapeDtypeStruct((B, 2 * M, W), F32))
    n, t, po, pi = pl.pallas_call(
        prep_kernel,
        out_shape=out,
        in_specs=[pl.BlockSpec(memory_space=pltpu.VMEM)] * 6,
        out_specs=[pl.BlockSpec(memory_space=pltpu.VMEM)] * 4,
        compiler_params=pltpu.CompilerParams(vmem_limit_bytes=min(8 * W // 128, 60) * 1024 * 1024),
        name="prep",
    )(go, bo, wn, gi, bi, ww)
    return n, ww, t, po, pi


def send_kernel(x_ref, out_ref):
    C, R, W = x_ref.shape
    pairs = out_ref.shape[0] // 2
    cols = W // pairs
    half = cols // 2
    x = x_ref[...].astype(F32)
    rows = lax.broadcasted_iota(jnp.int32, (W // 2, W), 0)
    lanes = lax.broadcasted_iota(jnp.int32, (W // 2, W), 1)
    for y in range(R):
        plane = x[:, y].astype(BF)
        parts = []
        for lo in range(2):
            pick = (lanes == 2 * rows + lo).astype(F32).astype(BF)
            parts.append(lax.dot_general(pick, plane, (((1,), (1,)), ((), ())), preferred_element_type=F32))
        both = jnp.concatenate(parts, axis=1).astype(BF)
        for q in range(pairs):
            for core in range(2):
                out_ref[2 * q + core, y * half:(y + 1) * half] = both[q * half:(q + 1) * half]


def join_kernel(recv_ref, x_ref, mate_ref, out_ref):
    n, r, lanes = recv_ref.shape
    C, R, W = x_ref.shape
    half = r // R
    recv = recv_ref[...].reshape(n * r, lanes)
    row = lax.broadcasted_iota(jnp.int32, (n * r, W), 0)
    col = lax.broadcasted_iota(jnp.int32, (n * r, W), 1)
    mine = x_ref[...].astype(F32)
    mate = mate_ref[...].astype(F32)
    first = lax.rem(lax.axis_index("row"), 2) == 0
    for p in range(half):
        pick = (row == col * half + p).astype(F32).astype(BF)
        part = lax.dot_general(recv, pick, (((0,), (0,)), ((), ())), preferred_element_type=F32)
        for lo in range(2):
            y = 2 * p + lo
            own = mine[:, y % R]
            other = mate[:, y % R]
            if y < R:
                straight = jnp.where(first, own, other)
            else:
                straight = jnp.where(first, other, own)
            out_ref[y] = ((straight + part[lo * C:(lo + 1) * C]) * 0.5).astype(BF)


def vmem_call(kernel, out_shape, args, name, mib):
    return pl.pallas_call(
        kernel,
        out_shape=out_shape,
        in_specs=[pl.BlockSpec(memory_space=pltpu.VMEM)] * len(args),
        out_specs=pl.BlockSpec(memory_space=pltpu.VMEM),
        compiler_params=pltpu.CompilerParams(vmem_limit_bytes=min(mib, 60) * 1024 * 1024),
        name=name,
    )(*args)


def body(features_in, gain_outer, bias_outer, w_narrow, gain_inner, bias_inner, w_widen):
    x = features_in
    C, R, part_cols = x.shape
    n = lax.axis_size("row")
    cols = lax.axis_size("col")
    if cols > 1:
        x = lax.all_gather(x, "col", axis=2, tiled=True)
    W = x.shape[2]
    side = R * n
    halo = 24
    ops = -(-halo // (2 * R))
    weights = prep(gain_outer, bias_outer, w_narrow, gain_inner, bias_inner, w_widen, W)

    swap = [(i, i ^ 1) for i in range(n)]
    mate = lax.ppermute(x, "row", swap)
    sent = vmem_call(send_kernel, jax.ShapeDtypeStruct((n, R * R, 2 * C), BF), [x], name="send", mib=4 * W // 128)
    recv = lax.all_to_all(sent, "row", split_axis=0, concat_axis=0, tiled=True)
    recv, weights = lax.optimization_barrier((recv, weights))
    own = vmem_call(join_kernel, jax.ShapeDtypeStruct((2 * R, C, W), BF), [recv, x, mate], name="join", mib=4 * W // 128 * W // 128)

    got = []
    for k in range(1, ops + 1):
        hop = [(i, i + 2 * k - 1) for i in range(n) if i % 2 == 1 and i + 2 * k - 1 < n]
        hop += [(i, i - 2 * k + 1) for i in range(n) if i % 2 == 0 and i - 2 * k + 1 >= 0]
        got.append(lax.ppermute(own, "row", hop))
    side_rows = jnp.concatenate(got, axis=0)
    other_rows = lax.ppermute(side_rows, "row", swap)
    out = net(own, side_rows, other_rows, *weights, R=R, side=side, halo=halo)
    if cols > 1:
        out = lax.dynamic_slice_in_dim(out, lax.axis_index("col") * part_cols, part_cols, axis=2)
    return out


def solution(mesh):
    in_specs = (P(None, ("groups", "row"), "col"), P(), P(), P(), P(), P(), P())
    out_specs = P(None, ("groups", "row"), "col")
    return jax.shard_map(body, mesh=mesh, in_specs=in_specs, out_specs=out_specs, check_vma=False)
```

time: 68.7 us -> 49.2 us (0.72)
  local copies, waits for them, and re-layouts: 15.3 us -> 4.66 us
  Pallas kernels: 26.7 us -> 18.6 us
  other arithmetic: 2.67 us -> 0 us
  waiting for transfers between devices: 6.32 us -> 7.77 us
    pallas_call x1 -> x2, Pallas kernels: 22.7 us -> 17.1 us  [the longest x1 16.5 us: net(): pl.pallas_call(functools.partial(net_kernel, R=R, side=side, halo=halo, l...]
    broadcast_in_dim x5 -> x0, local copies, waits for them, and re-layouts: 5.13 us -> none  [the longest x4 3.63 us: prep(): pk = lambda v: jnp.stack([v[:4], v[:4], v[4:]])[..., None]]
    another operation x3 -> x0, other arithmetic: 2.58 us -> none  [the longest x1 0.96 us: prep(): jnp.stack([n0[:4], n1, n0[4:]])]
    pallas_call x2, Pallas kernels: 3.96 us -> 1.54 us  [vmem_call(): pl.pallas_call(kernel, out_shape=out_shape, in_specs=[pl.BlockSpec(memory...]
    slice x7 -> x0, local copies, waits for them, and re-layouts: 1.81 us -> none  [the longest x3 0.89 us: prep(): n1 = n[:4].transpose(0, 2, 1, 3, 4).reshape(4, 3 * M, 3 * C)]
    ppermute x3, starting transfers between devices: 10.4 us -> 8.64 us  [body(): got.append(lax.ppermute(own, 'row', hop))]
    ppermute x1, starting transfers between devices: 0.07 us -> 1.85 us  [body(): other_rows = lax.ppermute(side_rows, 'row', swap)]
    transpose x3 -> x0, local copies, waits for them, and re-layouts: 1.71 us -> none  [the longest x1 1.52 us: body(): out = out.transpose(1, 0, 2)]
  transfers between devices with their start and end apart: 6 -> 6, of which waited for: 3 -> 4; matrix products, arithmetic and copies ran while one was open for 15% -> 0% of each run, Pallas kernels for 0% -> 1%
where the time goes in v2:
time: 49.2 us; the launch traced here: 48.4 us
  Pallas kernels  18.6 us (38%)
  starting transfers between devices  17.3 us (35%)
  waiting for transfers between devices  7.77 us (16%)
  local copies, waits for them, and re-layouts  4.66 us (9%)
    pallas_call x1, Pallas kernels, net(): pl.pallas_call(functools.partial(net_kernel, R=R, side=side, halo=halo, l...  16.5 us
    ppermute x3, starting transfers between devices, body(): got.append(lax.ppermute(own, 'row', hop))  8.64 us
    all_to_all x1, starting transfers between devices, body(): recv = lax.all_to_all(sent, 'row', split_axis=0, concat_axis=0, tiled=True)  6.35 us
    ppermute x3, waiting for transfers between devices, body(): got.append(lax.ppermute(own, 'row', hop))  4.99 us
    unnamed x18, local copies, waits for them, and re-layouts  4.64 us
    ppermute x1, starting transfers between devices, body(): other_rows = lax.ppermute(side_rows, 'row', swap)  1.85 us
    pallas_call x2, Pallas kernels, vmem_call(): pl.pallas_call(kernel, out_shape=out_shape, in_specs=[pl.BlockSpec(memory...  1.54 us
    all_to_all x1, waiting for transfers between devices, body(): recv = lax.all_to_all(sent, 'row', split_axis=0, concat_axis=0, tiled=True)  1.42 us
  transfers between devices with their start and end apart: 6, of which 4 were waited for; matrix products, arithmetic and copies ran while one was open for 0% of the time, Pallas kernels for 1%

profile of v2, /device:TPU:7, one launch (start us, length us, event | category | flops | bytes accessed | tf_op | source)
XLA Modules:
  0.0 48.4 jit_solution(6844203535332363921)
XLA Ops:
  0.0 0.0 copy-start
  0.0 0.0 copy-start.2
  0.0 0.9 %copy-done.2 = bf16[64,4,128]{2,1,0:T(4,128)(2,1)S(1)} copy-done((bf16[64,4,128]{2,1,0:T(4,128)(2,1)S(1)}, bf16[64,4,128]{2,1,0:T(4,128)(2,1)}, u32[]{:S(2)}) %copy-start.2) | copy-done | bytes 65560
  0.9 0.9 %send.1 = bf16[32,16,128]{2,1,0:T(8,128)(2,1)} custom-call(bf16[64,4,128]{2,1,0:T(4,128)(2,1)S(1)} %copy-done.2), custom_call_target="tpu_custom_call" | custom-call | tf_op jit(solution)/shard_map/send/pallas_call | solution.py:228
  1.8 0.0 copy-start.3
  1.8 6.4 %all-to-all-start = ((bf16[32,16,128]{2,1,0:T(8,128)(2,1)}), bf16[32,16,128]{2,1,0:T(8,128)(2,1)S(1)}, u32[]{:S(2)}, u32[]{:S(2)}) async-start(bf16[32,16,128]{2,1,0:T(8,128)(2,1)} %send.1), calls=%async_computation | async-start | bytes 262144 | tf_op jit(solution)/shard_map/all_to_all | solution.py:254
  8.2 0.0 copy-done.3
  8.2 0.5 collective-permute-start
  8.7 0.0 copy-done
  8.7 0.0 copy-start.1
  8.7 1.0 %copy-done.1 = bf16[8,32,576]{2,1,0:T(8,128)(2,1)S(1)} copy-done((bf16[8,32,576]{2,1,0:T(8,128)(2,1)S(1)}, bf16[8,32,576]{2,1,0:T(8,128)(2,1)}, u32[]{:S(2)}) %copy-start.1) | copy-done | bytes 294936
  9.6 0.0 copy-start.4
  9.6 0.7 %copy-done.4 = f32[8,64]{1,0:T(8,128)S(1)} copy-done((f32[8,64]{1,0:T(8,128)S(1)}, f32[8,64]{1,0:T(8,128)}, u32[]{:S(2)}) %copy-start.4) | copy-done | bytes 2072
  10.3 0.0 copy-start.5
  10.3 0.7 %copy-done.5 = f32[8,64]{1,0:T(8,128)S(1)} copy-done((f32[8,64]{1,0:T(8,128)S(1)}, f32[8,64]{1,0:T(8,128)}, u32[]{:S(2)}) %copy-start.5) | copy-done | bytes 2072
  11.0 0.0 copy-start.6
  11.0 0.7 %copy-done.6 = f32[8,32]{1,0:T(8,128)S(1)} copy-done((f32[8,32]{1,0:T(8,128)S(1)}, f32[8,32]{1,0:T(8,128)}, u32[]{:S(2)}) %copy-start.6) | copy-done | bytes 1048
  11.7 0.0 copy-start.7
  11.7 0.7 %copy-done.7 = f32[8,32]{1,0:T(8,128)S(1)} copy-done((f32[8,32]{1,0:T(8,128)S(1)}, f32[8,32]{1,0:T(8,128)}, u32[]{:S(2)}) %copy-start.7) | copy-done | bytes 1048
  12.4 0.5 %prep.1 = (bf16[12,96,192]{2,1,0:T(8,128)(2,1)S(1)}, bf16[8,64,288]{2,1,0:T(8,128)(2,1)S(1)}, f32[8,128,128]{2,1,0:T(8,128)S(1)}, f32[8,64,128]{2,1,0:T(8,128)S(1)}) custom-call(f32[8,64]{1,0:T(8,128)S(1)} %copy-done.4, f32[8,64]{1,0:T(8,128)S(1)} %copy-done.5, bf16[8,32,576]{2,1,0:T(8,128)(2,1)S(1)} %copy-done.1, f32[8,32]{1,0:T(8,128)S(1)} %copy-done.6, ...), custom_call_target="tpu_custom_call" | custom-call | tf_op jit(solution)/shard_map/prep/pallas_call | solution.py:172
  12.9 1.4 %all-to-all-done.recv_ref = bf16[32,16,128]{2,1,0:T(8,128)(2,1)S(1)} async-done(((bf16[32,16,128]{2,1,0:T(8,128)(2,1)}), bf16[32,16,128]{2,1,0:T(8,128)(2,1)S(1)}, u32[]{:S(2)}, u32[]{:S(2)}) %all-to-all-start) | async-done | bytes 131104 | tf_op jit(solution)/shard_map/all_to_all | solution.py:254
  14.4 0.0 collective-permute-done.mate_ref
  14.4 0.6 %join.1.own_ref = bf16[8,64,128]{2,1,0:T(8,128)(2,1)S(1)} custom-call(bf16[32,16,128]{2,1,0:T(8,128)(2,1)S(1)} %all-to-all-done.recv_ref, bf16[64,4,128]{2,1,0:T(4,128)(2,1)S(1)} %copy-done.3, bf16[64,4,128]{2,1,0:T(4,128)(2,1)S(1)} %collective-permute-done.mate_ref), custom_call_target="tpu_custom_call" | custom-call | tf_op jit(solution)/shard_map/join/pallas_call | solution.py:228
  15.0 4.3 %collective-permute-start.1 = (bf16[8,64,128]{2,1,0:T(8,128)(2,1)S(1)}, bf16[8,64,128]{2,1,0:T(8,128)(2,1)S(1)}, u32[]{:S(2)}, u32[]{:S(2)}) collective-permute-start(bf16[8,64,128]{2,1,0:T(8,128)(2,1)S(1)} %join.1.own_ref), channel_id=1, source_target_pairs={{1,2},{3,4},{5,6},{7,8},{9,10},{11,12},{13,14},{15,16},{17,18},{19... | collective-permute-start | bytes 393224 | tf_op jit(solution)/shard_map/ppermute | solution.py:262
  19.3 1.9 %collective-permute-start.2 = (bf16[8,64,128]{2,1,0:T(8,128)(2,1)S(1)}, bf16[8,64,128]{2,1,0:T(8,128)(2,1)S(1)}, u32[]{:S(2)}, u32[]{:S(2)}) collective-permute-start(bf16[8,64,128]{2,1,0:T(8,128)(2,1)S(1)} %join.1.own_ref), channel_id=1, source_target_pairs={{1,4},{3,6},{5,8},{7,10},{9,12},{11,14},{13,16},{15,18},{17,20},{1... | collective-permute-start | bytes 393224 | tf_op jit(solution)/shard_map/ppermute | solution.py:262
  21.2 2.4 %collective-permute-start.3 = (bf16[8,64,128]{2,1,0:T(8,128)(2,1)S(1)}, bf16[8,64,128]{2,1,0:T(8,128)(2,1)S(1)}, u32[]{:S(2)}, u32[]{:S(2)}) collective-permute-start(bf16[8,64,128]{2,1,0:T(8,128)(2,1)S(1)} %join.1.own_ref), channel_id=1, source_target_pairs={{1,6},{3,8},{5,10},{7,12},{9,14},{11,16},{13,18},{15,20},{17,22},{... | collective-permute-start | bytes 393224 | tf_op jit(solution)/shard_map/ppermute | solution.py:262
  23.6 0.0 collective-permute-done.1
  23.7 2.8 %collective-permute-done.2 = bf16[8,64,128]{2,1,0:T(8,128)(2,1)S(1)} collective-permute-done((bf16[8,64,128]{2,1,0:T(8,128)(2,1)S(1)}, bf16[8,64,128]{2,1,0:T(8,128)(2,1)S(1)}, u32[]{:S(2)}, u32[]{:S(2)}) %collective-permute-start.2) | collective-permute-done | bytes 131104 | tf_op jit(solution)/shard_map/ppermute | solution.py:262
  26.5 2.2 %collective-permute-done.3 = bf16[8,64,128]{2,1,0:T(8,128)(2,1)S(1)} collective-permute-done((bf16[8,64,128]{2,1,0:T(8,128)(2,1)S(1)}, bf16[8,64,128]{2,1,0:T(8,128)(2,1)S(1)}, u32[]{:S(2)}, u32[]{:S(2)}) %collective-permute-start.3) | collective-permute-done | bytes 131104 | tf_op jit(solution)/shard_map/ppermute | solution.py:262
  28.7 1.8 %collective-permute-start.4 = (bf16[24,64,128]{2,1,0:T(8,128)(2,1)S(1)}, bf16[24,64,128]{2,1,0:T(8,128)(2,1)S(1)}, u32[]{:S(2)}, u32[]{:S(2)}) collective-permute-start(bf16[24,64,128]{2,1,0:T(8,128)(2,1)S(1)} %constant_dynamic-update-slice_fusion.a_ref), channel_id=1, source_target_pairs={{0,1},{1,0},{2,3},{3,2},{4,5},{5,4},{6,7},{7,6},{8,9},{9,8},{10,11... | collective-permute-start | bytes 1179656 | tf_op jit(solution)/shard_map/ppermute | solution.py:264
  30.6 1.3 %collective-permute-done.4.b_ref = bf16[24,64,128]{2,1,0:T(8,128)(2,1)S(1)} collective-permute-done((bf16[24,64,128]{2,1,0:T(8,128)(2,1)S(1)}, bf16[24,64,128]{2,1,0:T(8,128)(2,1)S(1)}, u32[]{:S(2)}, u32[]{:S(2)}) %collective-permute-start.4) | collective-permute-done | bytes 393248 | tf_op jit(solution)/shard_map/ppermute | solution.py:264
  31.9 16.5 %net.1 = bf16[64,4,128]{2,1,0:T(4,128)(2,1)} custom-call(bf16[8,64,128]{2,1,0:T(8,128)(2,1)S(1)} %join.1.own_ref, bf16[24,64,128]{2,1,0:T(8,128)(2,1)S(1)} %constant_dynamic-update-slice_fusion.a_ref, bf16[24,64,128]{2,1,0:T(8,128)(2,1)S(1)} %collective-permute-done.4.b_ref, bf16[12,96,192]{2,1,0:T(8,128)(2,1)S(1)} %get-tuple-element.20.wn_ref, ...), custom_call_target="tpu_custom_call" | custom-call | tf_op jit(solution)/shard_map/net/pallas_call | solution.py:129
  (3 shorter events, 0.0 us)
Async XLA Ops:
  0.0 8.7 %copy-start = (bf16[8,64,288]{2,1,0:T(8,128)(2,1)S(1)}, bf16[8,64,288]{2,1,0:T(8,128)(2,1)}, u32[]{:S(2)}) copy-start(bf16[8,64,288]{2,1,0:T(8,128)(2,1)} %ww_ref.2) | copy-start | bytes 884740
  0.0 0.9 %copy-start.2 = (bf16[64,4,128]{2,1,0:T(4,128)(2,1)S(1)}, bf16[64,4,128]{2,1,0:T(4,128)(2,1)}, u32[]{:S(2)}) copy-start(bf16[64,4,128]{2,1,0:T(4,128)(2,1)} %x_ref.3) | copy-start | bytes 196612
  1.8 6.4 %copy-start.3 = (bf16[64,4,128]{2,1,0:T(4,128)(2,1)S(1)}, bf16[64,4,128]{2,1,0:T(4,128)(2,1)}, u32[]{:S(2)}) copy-start(bf16[64,4,128]{2,1,0:T(4,128)(2,1)} %x_ref.3) | copy-start | bytes 196612
  1.8 12.5 %all-to-all-start = ((bf16[32,16,128]{2,1,0:T(8,128)(2,1)}), bf16[32,16,128]{2,1,0:T(8,128)(2,1)S(1)}, u32[]{:S(2)}, u32[]{:S(2)}) async-start(bf16[32,16,128]{2,1,0:T(8,128)(2,1)} %send.1), calls=%async_computation | async-start | bytes 262144 | tf_op jit(solution)/shard_map/all_to_all | solution.py:254
  8.2 6.2 %collective-permute-start = (bf16[64,4,128]{2,1,0:T(4,128)(2,1)S(1)}, bf16[64,4,128]{2,1,0:T(4,128)(2,1)S(1)}, u32[]{:S(2)}, u32[]{:S(2)}) collective-permute-start(bf16[64,4,128]{2,1,0:T(4,128)(2,1)S(1)} %copy-done.3), channel_id=1, source_target_pairs={{0,1},{1,0},{2,3},{3,2},{4,5},{5,4},{6,7},{7,6},{8,9},{9,8},{10,11... | collective-permute-start | bytes 196616 | tf_op jit(solution)/shard_map/ppermute | solution.py:252
  8.7 1.0 %copy-start.1 = (bf16[8,32,576]{2,1,0:T(8,128)(2,1)S(1)}, bf16[8,32,576]{2,1,0:T(8,128)(2,1)}, u32[]{:S(2)}) copy-start(bf16[8,32,576]{2,1,0:T(8,128)(2,1)} %wn_ref.1) | copy-start | bytes 884740
  9.6 0.7 %copy-start.4 = (f32[8,64]{1,0:T(8,128)S(1)}, f32[8,64]{1,0:T(8,128)}, u32[]{:S(2)}) copy-start(f32[8,64]{1,0:T(8,128)} %go_ref.1) | copy-start | bytes 6148
  10.3 0.7 %copy-start.5 = (f32[8,64]{1,0:T(8,128)S(1)}, f32[8,64]{1,0:T(8,128)}, u32[]{:S(2)}) copy-start(f32[8,64]{1,0:T(8,128)} %bo_ref.1) | copy-start | bytes 6148
  11.0 0.7 %copy-start.6 = (f32[8,32]{1,0:T(8,128)S(1)}, f32[8,32]{1,0:T(8,128)}, u32[]{:S(2)}) copy-start(f32[8,32]{1,0:T(8,128)} %gi_ref.1) | copy-start | bytes 3076
  11.7 0.7 %copy-start.7 = (f32[8,32]{1,0:T(8,128)S(1)}, f32[8,32]{1,0:T(8,128)}, u32[]{:S(2)}) copy-start(f32[8,32]{1,0:T(8,128)} %bi_ref.1) | copy-start | bytes 3076
  15.0 8.7 %collective-permute-start.1 = (bf16[8,64,128]{2,1,0:T(8,128)(2,1)S(1)}, bf16[8,64,128]{2,1,0:T(8,128)(2,1)S(1)}, u32[]{:S(2)}, u32[]{:S(2)}) collective-permute-start(bf16[8,64,128]{2,1,0:T(8,128)(2,1)S(1)} %join.1.own_ref), channel_id=1, source_target_pairs={{1,2},{3,4},{5,6},{7,8},{9,10},{11,12},{13,14},{15,16},{17,18},{19... | collective-permute-start | bytes 393224 | tf_op jit(solution)/shard_map/ppermute | solution.py:262
  19.3 7.2 %collective-permute-start.2 = (bf16[8,64,128]{2,1,0:T(8,128)(2,1)S(1)}, bf16[8,64,128]{2,1,0:T(8,128)(2,1)S(1)}, u32[]{:S(2)}, u32[]{:S(2)}) collective-permute-start(bf16[8,64,128]{2,1,0:T(8,128)(2,1)S(1)} %join.1.own_ref), channel_id=1, source_target_pairs={{1,4},{3,6},{5,8},{7,10},{9,12},{11,14},{13,16},{15,18},{17,20},{1... | collective-permute-start | bytes 393224 | tf_op jit(solution)/shard_map/ppermute | solution.py:262
  21.2 7.5 %collective-permute-start.3 = (bf16[8,64,128]{2,1,0:T(8,128)(2,1)S(1)}, bf16[8,64,128]{2,1,0:T(8,128)(2,1)S(1)}, u32[]{:S(2)}, u32[]{:S(2)}) collective-permute-start(bf16[8,64,128]{2,1,0:T(8,128)(2,1)S(1)} %join.1.own_ref), channel_id=1, source_target_pairs={{1,6},{3,8},{5,10},{7,12},{9,14},{11,16},{13,18},{15,20},{17,22},{... | collective-permute-start | bytes 393224 | tf_op jit(solution)/shard_map/ppermute | solution.py:262
  28.7 3.2 %collective-permute-start.4 = (bf16[24,64,128]{2,1,0:T(8,128)(2,1)S(1)}, bf16[24,64,128]{2,1,0:T(8,128)(2,1)S(1)}, u32[]{:S(2)}, u32[]{:S(2)}) collective-permute-start(bf16[24,64,128]{2,1,0:T(8,128)(2,1)S(1)} %constant_dynamic-update-slice_fusion.a_ref), channel_id=1, source_target_pairs={{0,1},{1,0},{2,3},{3,2},{4,5},{5,4},{6,7},{7,6},{8,9},{9,8},{10,11... | collective-permute-start | bytes 1179656 | tf_op jit(solution)/shard_map/ppermute | solution.py:264

commit v3 on v2

v3 whole, which is shorter than its diff:
```python
import functools

import jax
import jax.numpy as jnp
from jax import lax
from jax.experimental import pallas as pl
from jax.experimental.pallas import tpu as pltpu
from jax.sharding import PartitionSpec as P

F32 = jnp.float32
BF = jnp.bfloat16
ROWS = 8
LAG = 1
GAP_A = 1
GAP_B = 1


def groups(n):
    return [(at, min(ROWS, n - at)) for at in range(0, n, ROWS)]


def schedule(n, lag):
    parts = []
    done = {}
    lo = 0
    clock = 0
    for j in range(4):
        d = 1 + j // 2
        for name, first, count, gap, late in (
            ("narrow", lo + d, n - 2 * d, GAP_A, 2), ("widen", lo + 2 * d, n - 4 * d, GAP_B, 1)):
            time = clock
            for at, rows in groups(count):
                y = first + at
                reads = range(y - d, y + rows + d)
                source = (j, "narrow") if name == "widen" else (j - 1, "widen")
                ready = max((done.get(source + (r,), -lag) for r in reads), default=0) + lag
                time = max(time + 1, ready)
                for part in range(late + 1):
                    parts.append((time + part * gap, -part, name == "narrow", len(parts), (j, y, rows, name, part)))
                for r in range(y, y + rows):
                    done[(j, name, r)] = time + late * gap
            if name == "narrow":
                clock = time
        lo, n = lo + 2 * d, n - 4 * d
    return [e[-1] for e in sorted(parts)]


def net_kernel(own_ref, far_ref, near_ref, other_ref, wn_ref, ww_ref, wt_ref, po_ref, pi_ref, out_ref,
               s_ref, t_ref, h_ref, i_ref, *, R, side, halo, lag):
    me = lax.axis_index("row")
    parity = lax.rem(me, 2)
    two = near_ref.shape[0]
    pairs = 3
    ext = pairs * two
    g0 = (me - parity) * R - ext
    W = own_ref.shape[-1]
    C = own_ref.shape[1]
    M = wn_ref.shape[1] // 3
    base = R
    shift = R - R * parity
    lane = lax.broadcasted_iota(jnp.int32, (1, W), 1)

    def valid(y):
        g = g0 + y - shift
        return (g >= 0) & (g < side)

    def right(h, d):
        return jnp.where(lane >= d, pltpu.roll(h, d, 1), jnp.zeros_like(h))

    def left(h, d):
        return jnp.where(lane < W - d, pltpu.roll(h, W - d, 1), jnp.zeros_like(h))

    def hidden(t, y, k):
        h = jnp.maximum(t + po_ref[k], 0.0).astype(BF)
        return jnp.where(valid(y), h, jnp.zeros_like(h))

    def run_pass(tb, lo, n, narrow_row, widen_of, block0):
        live = {}

        def narrow(j, y, rows):
            d = 1 + j // 2
            rhs = jnp.concatenate(
                [jnp.concatenate([h_ref[y + r + (k - 1) * d] for k in range(3)], axis=0) for r in range(rows)], axis=1)
            p = jnp.dot(wn_ref[narrow_row + j], rhs, preferred_element_type=F32)
            yield
            vs = []
            for r in range(rows):
                q = p[:, r * W:(r + 1) * W]
                v = right(q[0:M], d) + q[M:2 * M] + left(q[2 * M:3 * M], d)
                v = jnp.maximum(v + pi_ref[block0 + j], 0.0).astype(BF)
                vs.append(jnp.where(valid(y + r), v, jnp.zeros_like(v)))
            yield
            for r in range(rows):
                v = vs[r]
                i_ref[y + r, 0:M] = right(v, d)
                i_ref[y + r, M:2 * M] = v
                i_ref[y + r, 2 * M:3 * M] = left(v, d)

        def widen(j, y, rows):
            d = 1 + j // 2
            rhs = jnp.concatenate(
                [jnp.concatenate([i_ref[y + r + (k - 1) * d] for k in range(3)], axis=0) for r in range(rows)], axis=1)
            q = jnp.dot(widen_of(j), rhs, preferred_element_type=F32)
            yield
            for r in range(rows):
                old = s_ref[y + r] if j == 0 else t_ref[tb, y + r]
                t = old + q[:, r * W:(r + 1) * W]
                t_ref[tb, y + r] = t
                if j < 3:
                    h_ref[y + r] = hidden(t, y + r, block0 + j + 1)

        for j, y, rows, name, part in schedule(n, lag):
            key = (j, y, name)
            if part == 0:
                live[key] = (narrow if name == "narrow" else widen)(j, lo + y, rows)
            next(live[key], None)

    def place(offset, ref, first):
        at = (pairs + offset) * two + shift
        for i in range(two):
            s_ref[at + i] = ref[first + i].astype(F32)

    way = 2 * parity - 1
    place(0, own_ref, 0)
    place(way, own_ref, two)
    place(2 * way, far_ref, 0)
    place(3 * way, far_ref, two)
    place(-way, near_ref, 0)
    place(-2 * way, other_ref, 0)
    place(-3 * way, other_ref, two)

    @pl.loop(0, 2)
    def _(ps):
        for i in range(R + 2 * halo):
            h_ref[base + i] = hidden(s_ref[base + i], base + i, 0)
        run_pass(ps, base, R + 2 * halo, 4 * ps, lambda j: wt_ref[4 * ps + j], 0)
    mid = base + halo // 2
    for i in range(R + halo):
        t = (t_ref[0, mid + i] + t_ref[1, mid + i]) * 0.5
        s_ref[mid + i] = t
        h_ref[mid + i] = hidden(t, mid + i, 4)
    run_pass(0, mid, R + halo, 8, lambda j: ww_ref[4 + j], 4)
    for i in range(R):
        out_ref[:, i] = t_ref[0, base + halo + i].astype(BF)


def net(own, far, near, other, wn, ww, wt, po, pi, *, R, side, halo):
    two, C, W = near.shape
    win = 7 * two + R
    M = wn.shape[1] // 3
    full = lambda: pl.BlockSpec(memory_space=pltpu.VMEM)
    return pl.pallas_call(
        functools.partial(net_kernel, R=R, side=side, halo=halo, lag=LAG),
        out_shape=jax.ShapeDtypeStruct((C, R, W), BF),
        in_specs=[full() for _ in range(9)],
        out_specs=full(),
        scratch_shapes=[pltpu.VMEM((win, C, W), F32), pltpu.VMEM((2, win, C, W), F32),
                        pltpu.VMEM((win, C, W), BF), pltpu.VMEM((win, 3 * M, W), BF)],
        compiler_params=pltpu.CompilerParams(vmem_limit_bytes=min(15 * W // 128, 60) * 1024 * 1024),
        name="net",
    )(own, far, near, other, wn, ww, wt, po, pi)


def prep_kernel(go_ref, bo_ref, wn_ref, gi_ref, bi_ref, ww_ref, n_ref, t_ref, po_ref, pi_ref):
    B, C = go_ref.shape
    M = gi_ref.shape[1]
    W = po_ref.shape[2]
    half = B // 2
    go = go_ref[...]
    outer = (bo_ref[...] / go).T
    inner = bi_ref[...].T
    gain = gi_ref[...].T
    for k in range(B):
        row = k if k < half else k + half
        go3 = jnp.concatenate([go[k:k + 1]] * 9, axis=1)
        w = wn_ref[k].astype(F32) * gain[:, k:k + 1] * go3
        for kx in range(3):
            n_ref[row, kx * M:(kx + 1) * M] = jnp.concatenate(
                [w[:, (3 * ky + kx) * C:(3 * ky + kx + 1) * C] for ky in range(3)], axis=1).astype(BF)
            if k < half:
                n_ref[k + half, kx * M:(kx + 1) * M] = w[:, 3 * kx * C:3 * (kx + 1) * C].astype(BF)
        if k < half:
            v = ww_ref[k]
            t_ref[k] = v
            v = v.astype(F32)
            t_ref[k + half] = jnp.concatenate(
                [v[:, (3 * kx + ky) * M:(3 * kx + ky + 1) * M] for ky in range(3) for kx in range(3)], axis=1).astype(BF)
        po_ref[k] = jnp.broadcast_to(outer[:, k:k + 1], (C, W))
        pi_ref[k] = jnp.broadcast_to(inner[:, k:k + 1], (M, W))


def prep(go, bo, wn, gi, bi, ww, W=128):
    B, C = go.shape
    M = gi.shape[1]
    out = (jax.ShapeDtypeStruct((B + B // 2, 3 * M, 3 * C), BF), jax.ShapeDtypeStruct((B, C, 9 * M), BF),
           jax.ShapeDtypeStruct((B, C, W), F32), jax.ShapeDtypeStruct((B, M, W), F32))
    n, t, po, pi = pl.pallas_call(
        prep_kernel,
        out_shape=out,
        in_specs=[pl.BlockSpec(memory_space=pltpu.VMEM)] * 6,
        out_specs=[pl.BlockSpec(memory_space=pltpu.VMEM)] * 4,
        compiler_params=pltpu.CompilerParams(vmem_limit_bytes=min(8 * W // 128, 60) * 1024 * 1024),
        name="prep",
    )(go, bo, wn, gi, bi, ww)
    return n, ww, t, po, pi


def send_kernel(x_ref, out_ref):
    C, R, W = x_ref.shape
    pairs = out_ref.shape[0] // 2
    cols = W // pairs
    half = cols // 2
    block = R * half
    x = x_ref[...].astype(F32)
    rows = lax.broadcasted_iota(jnp.int32, (W // 2, W), 0)
    lanes = lax.broadcasted_iota(jnp.int32, (W // 2, W), 1)
    picks = [(lanes == 2 * rows + lo).astype(F32).astype(BF) for lo in range(2)]
    nothing = jnp.zeros((block, 2 * C), BF)
    out_ref[0, block:2 * block] = nothing
    out_ref[2 * pairs - 1, block:2 * block] = nothing
    for y in range(R):
        plane = x[:, y].astype(BF)
        parts = [lax.dot_general(pick, plane, (((1,), (1,)), ((), ())), preferred_element_type=F32) for pick in picks]
        both = jnp.concatenate(parts, axis=1).astype(BF)
        for q in range(pairs):
            piece = both[q * half:(q + 1) * half]
            at = y * half
            out_ref[2 * q, at:at + half] = piece
            out_ref[2 * q + 1, at:at + half] = piece
            if q + 1 < pairs:
                out_ref[2 * q + 2, block + at:block + at + half] = piece
            if q > 0:
                out_ref[2 * q - 1, block + at:block + at + half] = piece


def join_kernel(recv_ref, mine_ref, next_ref, out_ref, near_ref):
    n, r, lanes = recv_ref.shape
    _, C, R, W = mine_ref.shape
    block = r // 2
    half = block // R
    row = lax.broadcasted_iota(jnp.int32, (n * block, W), 0)
    col = lax.broadcasted_iota(jnp.int32, (n * block, W), 1)
    even = lax.rem(lax.axis_index("row"), 2) == 0
    picks = [(row == col * half + p).astype(F32).astype(BF) for p in range(half)]
    for which, rows_ref in enumerate((mine_ref, next_ref)):
        recv = recv_ref[:, which * block:(which + 1) * block].reshape(n * block, lanes)
        first = rows_ref[0].astype(F32)
        second = rows_ref[1].astype(F32)
        ahead = even if which == 0 else jnp.logical_not(even)
        for p in range(half):
            part = lax.dot_general(recv, picks[p], (((0,), (0,)), ((), ())), preferred_element_type=F32)
            for lo in range(2):
                y = 2 * p + lo
                a, b = first[:, y % R], second[:, y % R]
                straight = jnp.where(ahead, a, b) if y < R else jnp.where(ahead, b, a)
                out = ((straight + part[lo * C:(lo + 1) * C]) * 0.5).astype(BF)
                out_ref[which * 2 * R + y] = out
                if which == 1:
                    near_ref[y] = out


def vmem_call(kernel, out_shape, args, name, mib):
    return pl.pallas_call(
        kernel,
        out_shape=out_shape,
        in_specs=[pl.BlockSpec(memory_space=pltpu.VMEM)] * len(args),
        out_specs=jax.tree.map(lambda _: pl.BlockSpec(memory_space=pltpu.VMEM), out_shape),
        compiler_params=pltpu.CompilerParams(vmem_limit_bytes=min(mib, 60) * 1024 * 1024),
        name=name,
    )(*args)


def body(features_in, gain_outer, bias_outer, w_narrow, gain_inner, bias_inner, w_widen):
    x = features_in
    C, R, part_cols = x.shape
    n = lax.axis_size("row")
    cols = lax.axis_size("col")
    if cols > 1:
        x = lax.all_gather(x, "col", axis=2, tiled=True)
    W = x.shape[2]
    side = R * n
    halo = 24
    assert halo <= 6 * R and n % 2 == 0
    weights = prep(gain_outer, bias_outer, w_narrow, gain_inner, bias_inner, w_widen, W)

    swap = [(i, i ^ 1) for i in range(n)]
    beside = [(i, i + 1) for i in range(1, n - 1, 2)] + [(i, i - 1) for i in range(2, n, 2)]
    beyond = [(i, i + 4) for i in range(0, n - 4, 2)] + [(i, i - 4) for i in range(5, n, 2)]
    mate = lax.ppermute(x, "row", swap)
    mine = jnp.stack([x, mate])
    following = lax.ppermute(mine, "row", beside)
    sent = vmem_call(send_kernel, jax.ShapeDtypeStruct((n, 2 * R * R, 2 * C), BF), [x], name="send", mib=4 * W // 128)
    recv = lax.all_to_all(sent, "row", split_axis=0, concat_axis=0, tiled=True)
    recv, weights = lax.optimization_barrier((recv, weights))
    rows = lambda k: jax.ShapeDtypeStruct((k * R, C, W), BF)
    own, near = vmem_call(join_kernel, (rows(4), rows(2)), [recv, mine, following], name="join", mib=6 * W // 128 * W // 128)
    far = lax.ppermute(own, "row", beyond)
    near = lax.ppermute(near, "row", swap)
    other = lax.ppermute(far, "row", swap)
    out = net(own, far, near, other, *weights, R=R, side=side, halo=halo)
    if cols > 1:
        out = lax.dynamic_slice_in_dim(out, lax.axis_index("col") * part_cols, part_cols, axis=2)
    return out


def solution(mesh):
    in_specs = (P(None, ("groups", "row"), "col"), P(), P(), P(), P(), P(), P())
    out_specs = P(None, ("groups", "row"), "col")
    return jax.shard_map(body, mesh=mesh, in_specs=in_specs, out_specs=out_specs, check_vma=False)
```

time: 49.2 us -> 46.1 us (0.937)
  waiting for transfers between devices: 7.77 us -> 11.9 us
  local copies, waits for them, and re-layouts: 4.66 us -> 0.86 us
  Pallas kernels: 18.6 us -> 16.6 us
  starting transfers between devices: 17.3 us -> 15.8 us
    unnamed x18 -> x16, local copies, waits for them, and re-layouts: 4.64 us -> 0.86 us
    pallas_call x1, Pallas kernels: 16.5 us -> 13.8 us  [net(): pl.pallas_call(functools.partial(net_kernel, R=R, side=side, halo=halo, l...]
    all_to_all x1, waiting for transfers between devices: 1.42 us -> 3.05 us  [body(): recv = lax.all_to_all(sent, 'row', split_axis=0, concat_axis=0, tiled=True)]
    ppermute x4, waiting for transfers between devices: 6.34 us -> 7.93 us  [the longest x1 5.46 us: body(): far = lax.ppermute(own, 'row', beyond)]
    ppermute x4, starting transfers between devices: 10.5 us -> 8.99 us  [the longest x1 3.34 us: body(): following = lax.ppermute(mine, 'row', beside)]
    ppermute x1, waiting for transfers between devices: 0.01 us -> 0.9 us  [body(): mate = lax.ppermute(x, 'row', swap)]
    pallas_call x2, Pallas kernels: 1.54 us -> 2.04 us  [vmem_call(): pl.pallas_call(kernel, out_shape=out_shape, in_specs=[pl.BlockSpec(memory...]
  transfers between devices with their start and end apart: 6 -> 6, of which waited for: 4 -> 5; matrix products, arithmetic and copies ran while one was open for 0% -> 0% of each run, Pallas kernels for 1% -> 2%
where the time goes in v3:
time: 46.1 us; the launch traced here: 45.3 us
  Pallas kernels  16.6 us (36%)
  starting transfers between devices  15.8 us (34%)
  waiting for transfers between devices  11.9 us (26%)
  local copies, waits for them, and re-layouts  0.86 us (2%)
    pallas_call x1, Pallas kernels, net(): pl.pallas_call(functools.partial(net_kernel, R=R, side=side, halo=halo, l...  13.8 us
    all_to_all x1, starting transfers between devices, body(): recv = lax.all_to_all(sent, 'row', split_axis=0, concat_axis=0, tiled=True)  6.35 us
    ppermute x1, waiting for transfers between devices, body(): far = lax.ppermute(own, 'row', beyond)  5.46 us
    ppermute x1, starting transfers between devices, body(): following = lax.ppermute(mine, 'row', beside)  3.34 us
    all_to_all x1, waiting for transfers between devices, body(): recv = lax.all_to_all(sent, 'row', split_axis=0, concat_axis=0, tiled=True)  3.05 us
    ppermute x1, starting transfers between devices, body(): other = lax.ppermute(far, 'row', swap)  2.99 us
    ppermute x1, starting transfers between devices, body(): far = lax.ppermute(own, 'row', beyond)  2.65 us
    pallas_call x2, Pallas kernels, vmem_call(): pl.pallas_call(kernel, out_shape=out_shape, in_specs=[pl.BlockSpec(memory...  2.04 us
  transfers between devices with their start and end apart: 6, of which 5 were waited for; matrix products, arithmetic and copies ran while one was open for 0% of the time, Pallas kernels for 2%

profile of v3, /device:TPU:7, one launch (start us, length us, event | category | flops | bytes accessed | tf_op | source)
XLA Modules:
  0.0 45.3 jit_solution(1659501054908266694)
XLA Ops:
  0.0 0.0 copy-start.2
  0.0 0.8 %copy-done.2 = bf16[64,4,128]{2,1,0:T(4,128)(2,1)S(1)} copy-done((bf16[64,4,128]{2,1,0:T(4,128)(2,1)S(1)}, bf16[64,4,128]{2,1,0:T(4,128)(2,1)}, u32[]{:S(2)}) %copy-start.2) | copy-done | bytes 65560
  0.8 0.0 copy-start.3
  0.8 1.0 %send.1 = bf16[32,32,128]{2,1,0:T(8,128)(2,1)} custom-call(bf16[64,4,128]{2,1,0:T(4,128)(2,1)S(1)} %copy-done.2), custom_call_target="tpu_custom_call" | custom-call | tf_op jit(solution)/shard_map/send/pallas_call | solution.py:263
  1.8 0.0 copy-start
  1.8 0.0 copy-start.1
  1.8 6.4 %all-to-all-start = ((bf16[32,32,128]{2,1,0:T(8,128)(2,1)}), bf16[32,32,128]{2,1,0:T(8,128)(2,1)S(1)}, u32[]{:S(2)}, u32[]{:S(2)}) async-start(bf16[32,32,128]{2,1,0:T(8,128)(2,1)} %send.1), calls=%async_computation | async-start | bytes 524288 | tf_op jit(solution)/shard_map/all_to_all | solution.py:293
  8.2 0.0 copy-done.3
  8.2 0.5 %collective-permute-start = (bf16[64,4,128]{2,1,0:T(4,128)(2,1)S(1)}, bf16[64,4,128]{2,1,0:T(4,128)(2,1)S(1)}, u32[]{:S(2)}, u32[]{:S(2)}) collective-permute-start(bf16[64,4,128]{2,1,0:T(4,128)(2,1)S(1)} %copy-done.3), channel_id=1, source_target_pairs={{0,1},{1,0},{2,3},{3,2},{4,5},{5,4},{6,7},{7,6},{8,9},{9,8},{10,11... | collective-permute-start | bytes 196616 | tf_op jit(solution)/shard_map/ppermute | solution.py:289
  8.7 0.9 %collective-permute-done = bf16[64,4,128]{2,1,0:T(4,128)(2,1)S(1)} collective-permute-done((bf16[64,4,128]{2,1,0:T(4,128)(2,1)S(1)}, bf16[64,4,128]{2,1,0:T(4,128)(2,1)S(1)}, u32[]{:S(2)}, u32[]{:S(2)}) %collective-permute-start) | collective-permute-done | bytes 65568 | tf_op jit(solution)/shard_map/ppermute | solution.py:289
  9.6 0.0 copy-start.4
  9.6 0.0 copy-start.5
  9.6 0.0 copy-start.6
  9.6 0.0 copy-start.7
  9.6 0.1 pad_maximum_fusion.mine_ref
  9.7 3.3 %collective-permute-start.1 = (bf16[2,64,4,128]{3,2,1,0:T(4,128)(2,1)S(1)}, bf16[2,64,4,128]{3,2,1,0:T(4,128)(2,1)S(1)}, u32[]{:S(2)}, u32[]{:S(2)}) collective-permute-start(bf16[2,64,4,128]{3,2,1,0:T(4,128)(2,1)S(1)} %pad_maximum_fusion.mine_ref), channel_id=1, source_target_pairs={{1,2},{3,4},{5,6},{7,8},{9,10},{11,12},{13,14},{15,16},{17,18},{19... | collective-permute-start | bytes 393224 | tf_op jit(solution)/shard_map/ppermute | solution.py:291
  13.0 0.0 copy-done
  13.0 0.0 copy-done.1
  13.0 0.0 copy-done.4
  13.0 0.0 copy-done.5
  13.1 0.0 copy-done.6
  13.1 0.0 copy-done.7
  13.1 0.8 %prep.1 = (bf16[12,96,192]{2,1,0:T(8,128)(2,1)S(1)}, bf16[8,64,288]{2,1,0:T(8,128)(2,1)S(1)}, f32[8,64,128]{2,1,0:T(8,128)S(1)}, f32[8,32,128]{2,1,0:T(8,128)S(1)}) custom-call(f32[8,64]{1,0:T(8,128)S(1)} %copy-done.4, f32[8,64]{1,0:T(8,128)S(1)} %copy-done.5, bf16[8,32,576]{2,1,0:T(8,128)(2,1)S(1)} %copy-done.1, f32[8,32]{1,0:T(8,128)S(1)} %copy-done.6, ...), custom_call_target="tpu_custom_call" | custom-call | tf_op jit(solution)/shard_map/prep/pallas_call | solution.py:197
  13.9 3.0 %all-to-all-done.recv_ref = bf16[32,32,128]{2,1,0:T(8,128)(2,1)S(1)} async-done(((bf16[32,32,128]{2,1,0:T(8,128)(2,1)}), bf16[32,32,128]{2,1,0:T(8,128)(2,1)S(1)}, u32[]{:S(2)}, u32[]{:S(2)}) %all-to-all-start) | async-done | bytes 262176 | tf_op jit(solution)/shard_map/all_to_all | solution.py:293
  16.9 1.1 %collective-permute-done.1.next_ref = bf16[2,64,4,128]{3,2,1,0:T(4,128)(2,1)S(1)} collective-permute-done((bf16[2,64,4,128]{3,2,1,0:T(4,128)(2,1)S(1)}, bf16[2,64,4,128]{3,2,1,0:T(4,128)(2,1)S(1)}, u32[]{:S(2)}, u32[]{:S(2)}) %collective-permute-start.1) | collective-permute-done | bytes 131104 | tf_op jit(solution)/shard_map/ppermute | solution.py:291
  18.0 1.1 %join.1 = (bf16[16,64,128]{2,1,0:T(8,128)(2,1)S(1)}, bf16[8,64,128]{2,1,0:T(8,128)(2,1)S(1)}) custom-call(bf16[32,32,128]{2,1,0:T(8,128)(2,1)S(1)} %all-to-all-done.recv_ref, bf16[2,64,4,128]{3,2,1,0:T(4,128)(2,1)S(1)} %pad_maximum_fusion.mine_ref, bf16[2,64,4,128]{3,2,1,0:T(4,128)(2,1)S(1)} %collective-permute-done.1.next_ref), custom_call_target="tpu_custom_call" | custom-call | tf_op jit(solution)/shard_map/join/pallas_call | solution.py:263
  19.1 2.7 %collective-permute-start.2 = (bf16[16,64,128]{2,1,0:T(8,128)(2,1)S(1)}, bf16[16,64,128]{2,1,0:T(8,128)(2,1)S(1)}, u32[]{:S(2)}, u32[]{:S(2)}) collective-permute-start(bf16[16,64,128]{2,1,0:T(8,128)(2,1)S(1)} %get-tuple-element.22.own_ref), channel_id=1, source_target_pairs={{0,4},{2,6},{4,8},{6,10},{8,12},{10,14},{12,16},{14,18},{16,20},{1... | collective-permute-start | bytes 786440 | tf_op jit(solution)/shard_map/ppermute | solution.py:297
  21.8 5.5 %collective-permute-done.2.far_ref = bf16[16,64,128]{2,1,0:T(8,128)(2,1)S(1)} collective-permute-done((bf16[16,64,128]{2,1,0:T(8,128)(2,1)S(1)}, bf16[16,64,128]{2,1,0:T(8,128)(2,1)S(1)}, u32[]{:S(2)}, u32[]{:S(2)}) %collective-permute-start.2) | collective-permute-done | bytes 262176 | tf_op jit(solution)/shard_map/ppermute | solution.py:297
  27.2 3.0 %collective-permute-start.4 = (bf16[16,64,128]{2,1,0:T(8,128)(2,1)S(1)}, bf16[16,64,128]{2,1,0:T(8,128)(2,1)S(1)}, u32[]{:S(2)}, u32[]{:S(2)}) collective-permute-start(bf16[16,64,128]{2,1,0:T(8,128)(2,1)S(1)} %collective-permute-done.2.far_ref), channel_id=1, source_target_pairs={{0,1},{1,0},{2,3},{3,2},{4,5},{5,4},{6,7},{7,6},{8,9},{9,8},{10,11... | collective-permute-start | bytes 786440 | tf_op jit(solution)/shard_map/ppermute | solution.py:299
  30.2 0.0 collective-permute-start.3
  30.2 1.3 %collective-permute-done.3.near_ref = bf16[8,64,128]{2,1,0:T(8,128)(2,1)S(1)} collective-permute-done((bf16[8,64,128]{2,1,0:T(8,128)(2,1)S(1)}, bf16[8,64,128]{2,1,0:T(8,128)(2,1)S(1)}, u32[]{:S(2)}, u32[]{:S(2)}) %collective-permute-start.3) | collective-permute-done | bytes 131104 | tf_op jit(solution)/shard_map/ppermute | solution.py:298
  31.6 0.0 collective-permute-done.4.other_ref
  31.6 13.8 %net.1 = bf16[64,4,128]{2,1,0:T(4,128)(2,1)} custom-call(bf16[16,64,128]{2,1,0:T(8,128)(2,1)S(1)} %get-tuple-element.22.own_ref, bf16[16,64,128]{2,1,0:T(8,128)(2,1)S(1)} %collective-permute-done.2.far_ref, bf16[8,64,128]{2,1,0:T(8,128)(2,1)S(1)} %collective-permute-done.3.near_ref, bf16[16,64,128]{2,1,0:T(8,128)(2,1)S(1)} %collective-permute-done.4.other_ref, ...), custom_call_target="tpu_custom_call" | custom-call | tf_op jit(solution)/shard_map/net/pallas_call | solution.py:152
Async XLA Ops:
  0.0 0.8 %copy-start.2 = (bf16[64,4,128]{2,1,0:T(4,128)(2,1)S(1)}, bf16[64,4,128]{2,1,0:T(4,128)(2,1)}, u32[]{:S(2)}) copy-start(bf16[64,4,128]{2,1,0:T(4,128)(2,1)} %x_ref.1) | copy-start | bytes 196612
  0.8 7.4 %copy-start.3 = (bf16[64,4,128]{2,1,0:T(4,128)(2,1)S(1)}, bf16[64,4,128]{2,1,0:T(4,128)(2,1)}, u32[]{:S(2)}) copy-start(bf16[64,4,128]{2,1,0:T(4,128)(2,1)} %x_ref.1) | copy-start | bytes 196612
  1.8 11.2 %copy-start = (bf16[8,64,288]{2,1,0:T(8,128)(2,1)S(1)}, bf16[8,64,288]{2,1,0:T(8,128)(2,1)}, u32[]{:S(2)}) copy-start(bf16[8,64,288]{2,1,0:T(8,128)(2,1)} %ww_ref.2) | copy-start | bytes 884740
  1.8 11.2 %copy-start.1 = (bf16[8,32,576]{2,1,0:T(8,128)(2,1)S(1)}, bf16[8,32,576]{2,1,0:T(8,128)(2,1)}, u32[]{:S(2)}) copy-start(bf16[8,32,576]{2,1,0:T(8,128)(2,1)} %wn_ref.1) | copy-start | bytes 884740
  1.8 15.1 %all-to-all-start = ((bf16[32,32,128]{2,1,0:T(8,128)(2,1)}), bf16[32,32,128]{2,1,0:T(8,128)(2,1)S(1)}, u32[]{:S(2)}, u32[]{:S(2)}) async-start(bf16[32,32,128]{2,1,0:T(8,128)(2,1)} %send.1), calls=%async_computation | async-start | bytes 524288 | tf_op jit(solution)/shard_map/all_to_all | solution.py:293
  8.2 1.4 %collective-permute-start = (bf16[64,4,128]{2,1,0:T(4,128)(2,1)S(1)}, bf16[64,4,128]{2,1,0:T(4,128)(2,1)S(1)}, u32[]{:S(2)}, u32[]{:S(2)}) collective-permute-start(bf16[64,4,128]{2,1,0:T(4,128)(2,1)S(1)} %copy-done.3), channel_id=1, source_target_pairs={{0,1},{1,0},{2,3},{3,2},{4,5},{5,4},{6,7},{7,6},{8,9},{9,8},{10,11... | collective-permute-start | bytes 196616 | tf_op jit(solution)/shard_map/ppermute | solution.py:289
  9.6 3.5 %copy-start.4 = (f32[8,64]{1,0:T(8,128)S(1)}, f32[8,64]{1,0:T(8,128)}, u32[]{:S(2)}) copy-start(f32[8,64]{1,0:T(8,128)} %go_ref.1) | copy-start | bytes 6148
  9.6 3.5 %copy-start.5 = (f32[8,64]{1,0:T(8,128)S(1)}, f32[8,64]{1,0:T(8,128)}, u32[]{:S(2)}) copy-start(f32[8,64]{1,0:T(8,128)} %bo_ref.1) | copy-start | bytes 6148
  9.6 3.5 %copy-start.6 = (f32[8,32]{1,0:T(8,128)S(1)}, f32[8,32]{1,0:T(8,128)}, u32[]{:S(2)}) copy-start(f32[8,32]{1,0:T(8,128)} %gi_ref.1) | copy-start | bytes 3076
  9.6 3.5 %copy-start.7 = (f32[8,32]{1,0:T(8,128)S(1)}, f32[8,32]{1,0:T(8,128)}, u32[]{:S(2)}) copy-start(f32[8,32]{1,0:T(8,128)} %bi_ref.1) | copy-start | bytes 3076
  9.7 8.4 %collective-permute-start.1 = (bf16[2,64,4,128]{3,2,1,0:T(4,128)(2,1)S(1)}, bf16[2,64,4,128]{3,2,1,0:T(4,128)(2,1)S(1)}, u32[]{:S(2)}, u32[]{:S(2)}) collective-permute-start(bf16[2,64,4,128]{3,2,1,0:T(4,128)(2,1)S(1)} %pad_maximum_fusion.mine_ref), channel_id=1, source_target_pairs={{1,2},{3,4},{5,6},{7,8},{9,10},{11,12},{13,14},{15,16},{17,18},{19... | collective-permute-start | bytes 393224 | tf_op jit(solution)/shard_map/ppermute | solution.py:291
  19.1 8.1 %collective-permute-start.2 = (bf16[16,64,128]{2,1,0:T(8,128)(2,1)S(1)}, bf16[16,64,128]{2,1,0:T(8,128)(2,1)S(1)}, u32[]{:S(2)}, u32[]{:S(2)}) collective-permute-start(bf16[16,64,128]{2,1,0:T(8,128)(2,1)S(1)} %get-tuple-element.22.own_ref), channel_id=1, source_target_pairs={{0,4},{2,6},{4,8},{6,10},{8,12},{10,14},{12,16},{14,18},{16,20},{1... | collective-permute-start | bytes 786440 | tf_op jit(solution)/shard_map/ppermute | solution.py:297
  27.2 4.3 %collective-permute-start.4 = (bf16[16,64,128]{2,1,0:T(8,128)(2,1)S(1)}, bf16[16,64,128]{2,1,0:T(8,128)(2,1)S(1)}, u32[]{:S(2)}, u32[]{:S(2)}) collective-permute-start(bf16[16,64,128]{2,1,0:T(8,128)(2,1)S(1)} %collective-permute-done.2.far_ref), channel_id=1, source_target_pairs={{0,1},{1,0},{2,3},{3,2},{4,5},{5,4},{6,7},{7,6},{8,9},{9,8},{10,11... | collective-permute-start | bytes 786440 | tf_op jit(solution)/shard_map/ppermute | solution.py:299
  30.2 1.3 %collective-permute-start.3 = (bf16[8,64,128]{2,1,0:T(8,128)(2,1)S(1)}, bf16[8,64,128]{2,1,0:T(8,128)(2,1)S(1)}, u32[]{:S(2)}, u32[]{:S(2)}) collective-permute-start(bf16[8,64,128]{2,1,0:T(8,128)(2,1)S(1)} %get-tuple-element.23), channel_id=1, source_target_pairs={{0,1},{1,0},{2,3},{3,2},{4,5},{5,4},{6,7},{7,6},{8,9},{9,8},{10,11... | collective-permute-start | bytes 393224 | tf_op jit(solution)/shard_map/ppermute | solution.py:298

commit v4 on v3

--- a/solution.py
+++ b/solution.py
@@ -9,44 +9,60 @@
 
 F32 = jnp.float32
 BF = jnp.bfloat16
-ROWS = 8
-LAG = 1
-GAP_A = 1
-GAP_B = 1
-
-
-def groups(n):
-    return [(at, min(ROWS, n - at)) for at in range(0, n, ROWS)]
-
-
-def schedule(n, lag):
+ROWS, ROWS2 = 8, 4
+LAG = LAG2 = 1
+GAP_A = GAP_B = 1
+SKEW = 0
+
+
+def groups(n, rows):
+    return [(at, min(rows, n - at)) for at in range(0, n, rows)]
+
+
+def schedule(total, halo):
     parts = []
     done = {}
-    lo = 0
-    clock = 0
-    for j in range(4):
-        d = 1 + j // 2
-        for name, first, count, gap, late in (
-            ("narrow", lo + d, n - 2 * d, GAP_A, 2), ("widen", lo + 2 * d, n - 4 * d, GAP_B, 1)):
-            time = clock
-            for at, rows in groups(count):
-                y = first + at
-                reads = range(y - d, y + rows + d)
-                source = (j, "narrow") if name == "widen" else (j - 1, "widen")
-                ready = max((done.get(source + (r,), -lag) for r in reads), default=0) + lag
-                time = max(time + 1, ready)
-                for part in range(late + 1):
-                    parts.append((time + part * gap, -part, name == "narrow", len(parts), (j, y, rows, name, part)))
-                for r in range(y, y + rows):
-                    done[(j, name, r)] = time + late * gap
-            if name == "narrow":
-                clock = time
-        lo, n = lo + 2 * d, n - 4 * d
+    emitted = [0]
+
+    def put(time, which, j, name, y, rows, late, gap):
+        for part in range(late + 1):
+            parts.append((time + part * gap, -part, name == "narrow", emitted[0], (which, j, y, rows, name, part)))
+            emitted[0] += 1
+        for r in range(y, y + rows):
+            done[(which, j, name, r)] = time + late * gap
+
+    def run(which, lo, n, clock, size, lag):
+        for j in range(4):
+            d = 1 + j // 2
+            for name, first, count in (("narrow", lo + d, n - 2 * d), ("widen", lo + 2 * d, n - 4 * d)):
+                time = clock
+                for at, rows in groups(count, size):
+                    y = first + at
+                    source = (which, j, "narrow") if name == "widen" else (which, j - 1, "widen")
+                    ready = [done[source + (r,)] + lag for r in range(y - d, y + rows + d) if source + (r,) in done]
+                    time = max([time + 1] + ready)
+                    if name == "narrow":
+                        put(time, which, j, name, y, rows, 2, GAP_A)
+                    else:
+                        put(time, which, j, name, y, rows, 1, GAP_B)
+                if name == "narrow":
+                    clock = time
+            lo, n = lo + 2 * d, n - 4 * d
+
+    for which in range(2):
+        run(which, 0, total, which * SKEW, ROWS, LAG)
+    mid, n = halo // 2, total - halo
+    time = 0
+    for at, rows in groups(n, ROWS2):
+        y = mid + at
+        time = max([time + 1] + [done[(v, 3, "widen", r)] + 1 for v in range(2) for r in range(y, y + rows)])
+        put(time, 2, -1, "widen", y, rows, 0, 0)
+    run(2, mid, n, done[(2, -1, "widen", mid)], ROWS2, LAG2)
     return [e[-1] for e in sorted(parts)]
 
 
 def net_kernel(own_ref, far_ref, near_ref, other_ref, wn_ref, ww_ref, wt_ref, po_ref, pi_ref, out_ref,
-               s_ref, t_ref, h_ref, i_ref, *, R, side, halo, lag):
+               s_ref, t_ref, first_ref, h_ref, i_ref, *, R, side, halo):
     me = lax.axis_index("row")
     parity = lax.rem(me, 2)
     two = near_ref.shape[0]
@@ -74,46 +90,48 @@
         h = jnp.maximum(t + po_ref[k], 0.0).astype(BF)
         return jnp.where(valid(y), h, jnp.zeros_like(h))
 
-    def run_pass(tb, lo, n, narrow_row, widen_of, block0):
-        live = {}
-
-        def narrow(j, y, rows):
-            d = 1 + j // 2
-            rhs = jnp.concatenate(
-                [jnp.concatenate([h_ref[y + r + (k - 1) * d] for k in range(3)], axis=0) for r in range(rows)], axis=1)
-            p = jnp.dot(wn_ref[narrow_row + j], rhs, preferred_element_type=F32)
-            yield
-            vs = []
-            for r in range(rows):
-                q = p[:, r * W:(r + 1) * W]
-                v = right(q[0:M], d) + q[M:2 * M] + left(q[2 * M:3 * M], d)
-                v = jnp.maximum(v + pi_ref[block0 + j], 0.0).astype(BF)
-                vs.append(jnp.where(valid(y + r), v, jnp.zeros_like(v)))
-            yield
-            for r in range(rows):
-                v = vs[r]
-                i_ref[y + r, 0:M] = right(v, d)
-                i_ref[y + r, M:2 * M] = v
-                i_ref[y + r, 2 * M:3 * M] = left(v, d)
-
-        def widen(j, y, rows):
-            d = 1 + j // 2
-            rhs = jnp.concatenate(
-                [jnp.concatenate([i_ref[y + r + (k - 1) * d] for k in range(3)], axis=0) for r in range(rows)], axis=1)
-            q = jnp.dot(widen_of(j), rhs, preferred_element_type=F32)
-            yield
-            for r in range(rows):
-                old = s_ref[y + r] if j == 0 else t_ref[tb, y + r]
-                t = old + q[:, r * W:(r + 1) * W]
-                t_ref[tb, y + r] = t
-                if j < 3:
-                    h_ref[y + r] = hidden(t, y + r, block0 + j + 1)
-
-        for j, y, rows, name, part in schedule(n, lag):
-            key = (j, y, name)
-            if part == 0:
-                live[key] = (narrow if name == "narrow" else widen)(j, lo + y, rows)
-            next(live[key], None)
+    def narrow(which, j, y, rows):
+        d = 1 + j // 2
+        hid = first_ref if j == 0 and which < 2 else h_ref.at[which]
+        rhs = jnp.concatenate(
+            [jnp.concatenate([hid[y + r + (k - 1) * d] for k in range(3)], axis=0) for r in range(rows)], axis=1)
+        p = jnp.dot(wn_ref[4 * which + j], rhs, preferred_element_type=F32)
+        yield
+        vs = []
+        block = 4 * (which // 2) + j
+        for r in range(rows):
+            q = p[:, r * W:(r + 1) * W]
+            v = right(q[0:M], d) + q[M:2 * M] + left(q[2 * M:3 * M], d)
+            v = jnp.maximum(v + pi_ref[block], 0.0).astype(BF)
+            vs.append(jnp.where(valid(y + r), v, jnp.zeros_like(v)))
+        yield
+        for r in range(rows):
+            v = vs[r]
+            i_ref[which, y + r, 0:M] = right(v, d)
+            i_ref[which, y + r, M:2 * M] = v
+            i_ref[which, y + r, 2 * M:3 * M] = left(v, d)
+
+    def widen(which, j, y, rows):
+        d = 1 + j // 2
+        block = 4 * (which // 2) + j
+        rhs = jnp.concatenate(
+            [jnp.concatenate([i_ref[which, y + r + (k - 1) * d] for k in range(3)], axis=0) for r in range(rows)], axis=1)
+        taps = ww_ref[block] if which == 2 else wt_ref[4 * which + j]
+        q = jnp.dot(taps, rhs, preferred_element_type=F32)
+        yield
+        for r in range(rows):
+            old = s_ref[y + r] if j == 0 and which < 2 else t_ref[which, y + r]
+            t = old + q[:, r * W:(r + 1) * W]
+            t_ref[which, y + r] = t
+            if j < 3:
+                h_ref[which, y + r] = hidden(t, y + r, block + 1)
+
+    def average(which, j, y, rows):
+        for r in range(rows):
+            t = (t_ref[0, y + r] + t_ref[1, y + r]) * 0.5
+            t_ref[2, y + r] = t
+            h_ref[2, y + r] = hidden(t, y + r, 4)
+        yield
 
     def place(offset, ref, first):
         at = (pairs + offset) * two + shift
@@ -129,19 +147,17 @@
     place(-2 * way, other_ref, 0)
     place(-3 * way, other_ref, two)
 
-    @pl.loop(0, 2)
-    def _(ps):
-        for i in range(R + 2 * halo):
-            h_ref[base + i] = hidden(s_ref[base + i], base + i, 0)
-        run_pass(ps, base, R + 2 * halo, 4 * ps, lambda j: wt_ref[4 * ps + j], 0)
-    mid = base + halo // 2
-    for i in range(R + halo):
-        t = (t_ref[0, mid + i] + t_ref[1, mid + i]) * 0.5
-        s_ref[mid + i] = t
-        h_ref[mid + i] = hidden(t, mid + i, 4)
-    run_pass(0, mid, R + halo, 8, lambda j: ww_ref[4 + j], 4)
+    for i in range(R + 2 * halo):
+        first_ref[base + i] = hidden(s_ref[base + i], base + i, 0)
+    live = {}
+    for which, j, y, rows, name, part in schedule(R + 2 * halo, halo):
+        key = (which, j, y, name)
+        if part == 0:
+            step = average if j < 0 else narrow if name == "narrow" else widen
+            live[key] = step(which, j, base + y, rows)
+        next(live[key], None)
     for i in range(R):
-        out_ref[:, i] = t_ref[0, base + halo + i].astype(BF)
+        out_ref[:, i] = t_ref[2, base + halo + i].astype(BF)
 
 
 def net(own, far, near, other, wn, ww, wt, po, pi, *, R, side, halo):
@@ -150,13 +166,13 @@
     M = wn.shape[1] // 3
     full = lambda: pl.BlockSpec(memory_space=pltpu.VMEM)
     return pl.pallas_call(
-        functools.partial(net_kernel, R=R, side=side, halo=halo, lag=LAG),
+        functools.partial(net_kernel, R=R, side=side, halo=halo),
         out_shape=jax.ShapeDtypeStruct((C, R, W), BF),
         in_specs=[full() for _ in range(9)],
         out_specs=full(),
-        scratch_shapes=[pltpu.VMEM((win, C, W), F32), pltpu.VMEM((2, win, C, W), F32),
-                        pltpu.VMEM((win, C, W), BF), pltpu.VMEM((win, 3 * M, W), BF)],
-        compiler_params=pltpu.CompilerParams(vmem_limit_bytes=min(15 * W // 128, 60) * 1024 * 1024),
+        scratch_shapes=[pltpu.VMEM((win, C, W), F32), pltpu.VMEM((3, win, C, W), F32), pltpu.VMEM((win, C, W), BF),
+                        pltpu.VMEM((3, win, C, W), BF), pltpu.VMEM((3, win, 3 * M, W), BF)],
+        compiler_params=pltpu.CompilerParams(vmem_limit_bytes=min(20 * W // 128, 60) * 1024 * 1024),
         name="net",
     )(own, far, near, other, wn, ww, wt, po, pi)
 

time: 46.1 us -> 45.1 us (0.978)
  Pallas kernels: 16.6 us -> 15.5 us
    pallas_call x1, Pallas kernels: 13.8 us -> 12.7 us  [net(): pl.pallas_call(functools.partial(net_kernel, R=R, side=side, halo=halo),...]
where the time goes in v4:
time: 45.1 us; the launch traced here: 44.3 us
  starting transfers between devices  16 us (35%)
  Pallas kernels  15.5 us (34%)
  waiting for transfers between devices  11.7 us (26%)
  local copies, waits for them, and re-layouts  0.86 us (2%)
    pallas_call x1, Pallas kernels, net(): pl.pallas_call(functools.partial(net_kernel, R=R, side=side, halo=halo),...  12.7 us
    all_to_all x1, starting transfers between devices, body(): recv = lax.all_to_all(sent, 'row', split_axis=0, concat_axis=0, tiled=True)  6.35 us
    ppermute x1, waiting for transfers between devices, body(): far = lax.ppermute(own, 'row', beyond)  5.28 us
    ppermute x1, starting transfers between devices, body(): following = lax.ppermute(mine, 'row', beside)  3.34 us
    all_to_all x1, waiting for transfers between devices, body(): recv = lax.all_to_all(sent, 'row', split_axis=0, concat_axis=0, tiled=True)  3.05 us
    ppermute x1, starting transfers between devices, body(): other = lax.ppermute(far, 'row', swap)  2.99 us
    ppermute x1, starting transfers between devices, body(): far = lax.ppermute(own, 'row', beyond)  2.83 us
    pallas_call x2, Pallas kernels, vmem_call(): pl.pallas_call(kernel, out_shape=out_shape, in_specs=[pl.BlockSpec(memory...  2.05 us
  transfers between devices with their start and end apart: 6, of which 5 were waited for; matrix products, arithmetic and copies ran while one was open for 0% of the time, Pallas kernels for 2%

profile of v4, /device:TPU:7, one launch (start us, length us, event | category | flops | bytes accessed | tf_op | source)
XLA Modules:
  0.0 44.3 jit_solution(8629242071514702379)
XLA Ops:
  0.0 0.0 copy-start.2
  0.0 0.8 %copy-done.2 = bf16[64,4,128]{2,1,0:T(4,128)(2,1)S(1)} copy-done((bf16[64,4,128]{2,1,0:T(4,128)(2,1)S(1)}, bf16[64,4,128]{2,1,0:T(4,128)(2,1)}, u32[]{:S(2)}) %copy-start.2) | copy-done | bytes 65560
  0.8 0.0 copy-start.3
  0.8 1.0 %send.1 = bf16[32,32,128]{2,1,0:T(8,128)(2,1)} custom-call(bf16[64,4,128]{2,1,0:T(4,128)(2,1)S(1)} %copy-done.2), custom_call_target="tpu_custom_call" | custom-call | tf_op jit(solution)/shard_map/send/pallas_call | solution.py:279
  1.8 0.0 copy-start
  1.8 0.0 copy-start.1
  1.8 6.4 %all-to-all-start = ((bf16[32,32,128]{2,1,0:T(8,128)(2,1)}), bf16[32,32,128]{2,1,0:T(8,128)(2,1)S(1)}, u32[]{:S(2)}, u32[]{:S(2)}) async-start(bf16[32,32,128]{2,1,0:T(8,128)(2,1)} %send.1), calls=%async_computation | async-start | bytes 524288 | tf_op jit(solution)/shard_map/all_to_all | solution.py:309
  8.2 0.0 copy-done.3
  8.2 0.5 %collective-permute-start = (bf16[64,4,128]{2,1,0:T(4,128)(2,1)S(1)}, bf16[64,4,128]{2,1,0:T(4,128)(2,1)S(1)}, u32[]{:S(2)}, u32[]{:S(2)}) collective-permute-start(bf16[64,4,128]{2,1,0:T(4,128)(2,1)S(1)} %copy-done.3), channel_id=1, source_target_pairs={{0,1},{1,0},{2,3},{3,2},{4,5},{5,4},{6,7},{7,6},{8,9},{9,8},{10,11... | collective-permute-start | bytes 196616 | tf_op jit(solution)/shard_map/ppermute | solution.py:305
  8.7 0.9 %collective-permute-done = bf16[64,4,128]{2,1,0:T(4,128)(2,1)S(1)} collective-permute-done((bf16[64,4,128]{2,1,0:T(4,128)(2,1)S(1)}, bf16[64,4,128]{2,1,0:T(4,128)(2,1)S(1)}, u32[]{:S(2)}, u32[]{:S(2)}) %collective-permute-start) | collective-permute-done | bytes 65568 | tf_op jit(solution)/shard_map/ppermute | solution.py:305
  9.6 0.0 copy-start.4
  9.6 0.0 copy-start.5
  9.6 0.0 copy-start.6
  9.6 0.0 copy-start.7
  9.6 0.1 pad_maximum_fusion.mine_ref
  9.7 3.3 %collective-permute-start.1 = (bf16[2,64,4,128]{3,2,1,0:T(4,128)(2,1)S(1)}, bf16[2,64,4,128]{3,2,1,0:T(4,128)(2,1)S(1)}, u32[]{:S(2)}, u32[]{:S(2)}) collective-permute-start(bf16[2,64,4,128]{3,2,1,0:T(4,128)(2,1)S(1)} %pad_maximum_fusion.mine_ref), channel_id=1, source_target_pairs={{1,2},{3,4},{5,6},{7,8},{9,10},{11,12},{13,14},{15,16},{17,18},{19... | collective-permute-start | bytes 393224 | tf_op jit(solution)/shard_map/ppermute | solution.py:307
  13.0 0.0 copy-done
  13.0 0.0 copy-done.1
  13.0 0.0 copy-done.4
  13.0 0.0 copy-done.5
  13.1 0.0 copy-done.6
  13.1 0.0 copy-done.7
  13.1 0.8 %prep.1 = (bf16[12,96,192]{2,1,0:T(8,128)(2,1)S(1)}, bf16[8,64,288]{2,1,0:T(8,128)(2,1)S(1)}, f32[8,64,128]{2,1,0:T(8,128)S(1)}, f32[8,32,128]{2,1,0:T(8,128)S(1)}) custom-call(f32[8,64]{1,0:T(8,128)S(1)} %copy-done.4, f32[8,64]{1,0:T(8,128)S(1)} %copy-done.5, bf16[8,32,576]{2,1,0:T(8,128)(2,1)S(1)} %copy-done.1, f32[8,32]{1,0:T(8,128)S(1)} %copy-done.6, ...), custom_call_target="tpu_custom_call" | custom-call | tf_op jit(solution)/shard_map/prep/pallas_call | solution.py:213
  13.9 3.0 %all-to-all-done.recv_ref = bf16[32,32,128]{2,1,0:T(8,128)(2,1)S(1)} async-done(((bf16[32,32,128]{2,1,0:T(8,128)(2,1)}), bf16[32,32,128]{2,1,0:T(8,128)(2,1)S(1)}, u32[]{:S(2)}, u32[]{:S(2)}) %all-to-all-start) | async-done | bytes 262176 | tf_op jit(solution)/shard_map/all_to_all | solution.py:309
  16.9 1.1 %collective-permute-done.1.next_ref = bf16[2,64,4,128]{3,2,1,0:T(4,128)(2,1)S(1)} collective-permute-done((bf16[2,64,4,128]{3,2,1,0:T(4,128)(2,1)S(1)}, bf16[2,64,4,128]{3,2,1,0:T(4,128)(2,1)S(1)}, u32[]{:S(2)}, u32[]{:S(2)}) %collective-permute-start.1) | collective-permute-done | bytes 131104 | tf_op jit(solution)/shard_map/ppermute | solution.py:307
  18.0 1.1 %join.1 = (bf16[16,64,128]{2,1,0:T(8,128)(2,1)S(1)}, bf16[8,64,128]{2,1,0:T(8,128)(2,1)S(1)}) custom-call(bf16[32,32,128]{2,1,0:T(8,128)(2,1)S(1)} %all-to-all-done.recv_ref, bf16[2,64,4,128]{3,2,1,0:T(4,128)(2,1)S(1)} %pad_maximum_fusion.mine_ref, bf16[2,64,4,128]{3,2,1,0:T(4,128)(2,1)S(1)} %collective-permute-done.1.next_ref), custom_call_target="tpu_custom_call" | custom-call | tf_op jit(solution)/shard_map/join/pallas_call | solution.py:279
  19.1 2.8 %collective-permute-start.2 = (bf16[16,64,128]{2,1,0:T(8,128)(2,1)S(1)}, bf16[16,64,128]{2,1,0:T(8,128)(2,1)S(1)}, u32[]{:S(2)}, u32[]{:S(2)}) collective-permute-start(bf16[16,64,128]{2,1,0:T(8,128)(2,1)S(1)} %get-tuple-element.22.own_ref), channel_id=1, source_target_pairs={{0,4},{2,6},{4,8},{6,10},{8,12},{10,14},{12,16},{14,18},{16,20},{1... | collective-permute-start | bytes 786440 | tf_op jit(solution)/shard_map/ppermute | solution.py:313
  21.9 5.3 %collective-permute-done.2.far_ref = bf16[16,64,128]{2,1,0:T(8,128)(2,1)S(1)} collective-permute-done((bf16[16,64,128]{2,1,0:T(8,128)(2,1)S(1)}, bf16[16,64,128]{2,1,0:T(8,128)(2,1)S(1)}, u32[]{:S(2)}, u32[]{:S(2)}) %collective-permute-start.2) | collective-permute-done | bytes 262176 | tf_op jit(solution)/shard_map/ppermute | solution.py:313
  27.2 3.0 %collective-permute-start.4 = (bf16[16,64,128]{2,1,0:T(8,128)(2,1)S(1)}, bf16[16,64,128]{2,1,0:T(8,128)(2,1)S(1)}, u32[]{:S(2)}, u32[]{:S(2)}) collective-permute-start(bf16[16,64,128]{2,1,0:T(8,128)(2,1)S(1)} %collective-permute-done.2.far_ref), channel_id=1, source_target_pairs={{0,1},{1,0},{2,3},{3,2},{4,5},{5,4},{6,7},{7,6},{8,9},{9,8},{10,11... | collective-permute-start | bytes 786440 | tf_op jit(solution)/shard_map/ppermute | solution.py:315
  30.2 0.0 collective-permute-start.3
  30.2 1.3 %collective-permute-done.3.near_ref = bf16[8,64,128]{2,1,0:T(8,128)(2,1)S(1)} collective-permute-done((bf16[8,64,128]{2,1,0:T(8,128)(2,1)S(1)}, bf16[8,64,128]{2,1,0:T(8,128)(2,1)S(1)}, u32[]{:S(2)}, u32[]{:S(2)}) %collective-permute-start.3) | collective-permute-done | bytes 131104 | tf_op jit(solution)/shard_map/ppermute | solution.py:314
  31.6 0.0 collective-permute-done.4.other_ref
  31.6 12.7 %net.1 = bf16[64,4,128]{2,1,0:T(4,128)(2,1)} custom-call(bf16[16,64,128]{2,1,0:T(8,128)(2,1)S(1)} %get-tuple-element.22.own_ref, bf16[16,64,128]{2,1,0:T(8,128)(2,1)S(1)} %collective-permute-done.2.far_ref, bf16[8,64,128]{2,1,0:T(8,128)(2,1)S(1)} %collective-permute-done.3.near_ref, bf16[16,64,128]{2,1,0:T(8,128)(2,1)S(1)} %collective-permute-done.4.other_ref, ...), custom_call_target="tpu_custom_call" | custom-call | tf_op jit(solution)/shard_map/net/pallas_call | solution.py:168
Async XLA Ops:
  0.0 0.8 %copy-start.2 = (bf16[64,4,128]{2,1,0:T(4,128)(2,1)S(1)}, bf16[64,4,128]{2,1,0:T(4,128)(2,1)}, u32[]{:S(2)}) copy-start(bf16[64,4,128]{2,1,0:T(4,128)(2,1)} %x_ref.1) | copy-start | bytes 196612
  0.8 7.4 %copy-start.3 = (bf16[64,4,128]{2,1,0:T(4,128)(2,1)S(1)}, bf16[64,4,128]{2,1,0:T(4,128)(2,1)}, u32[]{:S(2)}) copy-start(bf16[64,4,128]{2,1,0:T(4,128)(2,1)} %x_ref.1) | copy-start | bytes 196612
  1.8 11.2 %copy-start = (bf16[8,64,288]{2,1,0:T(8,128)(2,1)S(1)}, bf16[8,64,288]{2,1,0:T(8,128)(2,1)}, u32[]{:S(2)}) copy-start(bf16[8,64,288]{2,1,0:T(8,128)(2,1)} %ww_ref.2) | copy-start | bytes 884740
  1.8 11.2 %copy-start.1 = (bf16[8,32,576]{2,1,0:T(8,128)(2,1)S(1)}, bf16[8,32,576]{2,1,0:T(8,128)(2,1)}, u32[]{:S(2)}) copy-start(bf16[8,32,576]{2,1,0:T(8,128)(2,1)} %wn_ref.1) | copy-start | bytes 884740
  1.8 15.1 %all-to-all-start = ((bf16[32,32,128]{2,1,0:T(8,128)(2,1)}), bf16[32,32,128]{2,1,0:T(8,128)(2,1)S(1)}, u32[]{:S(2)}, u32[]{:S(2)}) async-start(bf16[32,32,128]{2,1,0:T(8,128)(2,1)} %send.1), calls=%async_computation | async-start | bytes 524288 | tf_op jit(solution)/shard_map/all_to_all | solution.py:309
  8.2 1.4 %collective-permute-start = (bf16[64,4,128]{2,1,0:T(4,128)(2,1)S(1)}, bf16[64,4,128]{2,1,0:T(4,128)(2,1)S(1)}, u32[]{:S(2)}, u32[]{:S(2)}) collective-permute-start(bf16[64,4,128]{2,1,0:T(4,128)(2,1)S(1)} %copy-done.3), channel_id=1, source_target_pairs={{0,1},{1,0},{2,3},{3,2},{4,5},{5,4},{6,7},{7,6},{8,9},{9,8},{10,11... | collective-permute-start | bytes 196616 | tf_op jit(solution)/shard_map/ppermute | solution.py:305
  9.6 3.5 %copy-start.4 = (f32[8,64]{1,0:T(8,128)S(1)}, f32[8,64]{1,0:T(8,128)}, u32[]{:S(2)}) copy-start(f32[8,64]{1,0:T(8,128)} %go_ref.1) | copy-start | bytes 6148
  9.6 3.5 %copy-start.5 = (f32[8,64]{1,0:T(8,128)S(1)}, f32[8,64]{1,0:T(8,128)}, u32[]{:S(2)}) copy-start(f32[8,64]{1,0:T(8,128)} %bo_ref.1) | copy-start | bytes 6148
  9.6 3.5 %copy-start.6 = (f32[8,32]{1,0:T(8,128)S(1)}, f32[8,32]{1,0:T(8,128)}, u32[]{:S(2)}) copy-start(f32[8,32]{1,0:T(8,128)} %gi_ref.1) | copy-start | bytes 3076
  9.6 3.5 %copy-start.7 = (f32[8,32]{1,0:T(8,128)S(1)}, f32[8,32]{1,0:T(8,128)}, u32[]{:S(2)}) copy-start(f32[8,32]{1,0:T(8,128)} %bi_ref.1) | copy-start | bytes 3076
  9.7 8.4 %collective-permute-start.1 = (bf16[2,64,4,128]{3,2,1,0:T(4,128)(2,1)S(1)}, bf16[2,64,4,128]{3,2,1,0:T(4,128)(2,1)S(1)}, u32[]{:S(2)}, u32[]{:S(2)}) collective-permute-start(bf16[2,64,4,128]{3,2,1,0:T(4,128)(2,1)S(1)} %pad_maximum_fusion.mine_ref), channel_id=1, source_target_pairs={{1,2},{3,4},{5,6},{7,8},{9,10},{11,12},{13,14},{15,16},{17,18},{19... | collective-permute-start | bytes 393224 | tf_op jit(solution)/shard_map/ppermute | solution.py:307
  19.1 8.1 %collective-permute-start.2 = (bf16[16,64,128]{2,1,0:T(8,128)(2,1)S(1)}, bf16[16,64,128]{2,1,0:T(8,128)(2,1)S(1)}, u32[]{:S(2)}, u32[]{:S(2)}) collective-permute-start(bf16[16,64,128]{2,1,0:T(8,128)(2,1)S(1)} %get-tuple-element.22.own_ref), channel_id=1, source_target_pairs={{0,4},{2,6},{4,8},{6,10},{8,12},{10,14},{12,16},{14,18},{16,20},{1... | collective-permute-start | bytes 786440 | tf_op jit(solution)/shard_map/ppermute | solution.py:313
  27.2 4.3 %collective-permute-start.4 = (bf16[16,64,128]{2,1,0:T(8,128)(2,1)S(1)}, bf16[16,64,128]{2,1,0:T(8,128)(2,1)S(1)}, u32[]{:S(2)}, u32[]{:S(2)}) collective-permute-start(bf16[16,64,128]{2,1,0:T(8,128)(2,1)S(1)} %collective-permute-done.2.far_ref), channel_id=1, source_target_pairs={{0,1},{1,0},{2,3},{3,2},{4,5},{5,4},{6,7},{7,6},{8,9},{9,8},{10,11... | collective-permute-start | bytes 786440 | tf_op jit(solution)/shard_map/ppermute | solution.py:315
  30.2 1.3 %collective-permute-start.3 = (bf16[8,64,128]{2,1,0:T(8,128)(2,1)S(1)}, bf16[8,64,128]{2,1,0:T(8,128)(2,1)S(1)}, u32[]{:S(2)}, u32[]{:S(2)}) collective-permute-start(bf16[8,64,128]{2,1,0:T(8,128)(2,1)S(1)} %get-tuple-element.23), channel_id=1, source_target_pairs={{0,1},{1,0},{2,3},{3,2},{4,5},{5,4},{6,7},{7,6},{8,9},{9,8},{10,11... | collective-permute-start | bytes 393224 | tf_op jit(solution)/shard_map/ppermute | solution.py:314

commit v5 on v4

--- a/solution.py
+++ b/solution.py
@@ -6,6 +6,7 @@
 from jax.experimental import pallas as pl
 from jax.experimental.pallas import tpu as pltpu
 from jax.sharding import PartitionSpec as P
+
 
 F32 = jnp.float32
 BF = jnp.bfloat16
@@ -70,7 +71,6 @@
     ext = pairs * two
     g0 = (me - parity) * R - ext
     W = own_ref.shape[-1]
-    C = own_ref.shape[1]
     M = wn_ref.shape[1] // 3
     base = R
     shift = R - R * parity
@@ -275,14 +275,13 @@
                     near_ref[y] = out
 
 
-def vmem_call(kernel, out_shape, args, name, mib):
+def vmem_call(kernel, out_shape, args, mib):
     return pl.pallas_call(
         kernel,
         out_shape=out_shape,
         in_specs=[pl.BlockSpec(memory_space=pltpu.VMEM)] * len(args),
         out_specs=jax.tree.map(lambda _: pl.BlockSpec(memory_space=pltpu.VMEM), out_shape),
         compiler_params=pltpu.CompilerParams(vmem_limit_bytes=min(mib, 60) * 1024 * 1024),
-        name=name,
     )(*args)
 
 
@@ -305,11 +304,11 @@
     mate = lax.ppermute(x, "row", swap)
     mine = jnp.stack([x, mate])
     following = lax.ppermute(mine, "row", beside)
-    sent = vmem_call(send_kernel, jax.ShapeDtypeStruct((n, 2 * R * R, 2 * C), BF), [x], name="send", mib=4 * W // 128)
+    sent = vmem_call(send_kernel, jax.ShapeDtypeStruct((n, 2 * R * R, 2 * C), BF), [x], mib=4 * W // 128)
     recv = lax.all_to_all(sent, "row", split_axis=0, concat_axis=0, tiled=True)
     recv, weights = lax.optimization_barrier((recv, weights))
     rows = lambda k: jax.ShapeDtypeStruct((k * R, C, W), BF)
-    own, near = vmem_call(join_kernel, (rows(4), rows(2)), [recv, mine, following], name="join", mib=6 * W // 128 * W // 128)
+    own, near = vmem_call(join_kernel, (rows(4), rows(2)), [recv, mine, following], mib=6 * W // 128 * W // 128)
     far = lax.ppermute(own, "row", beyond)
     near = lax.ppermute(near, "row", swap)
     other = lax.ppermute(far, "row", swap)

time: 45.1 us -> 45.1 us (level)
  no operation moved by 1% of the time
where the time goes in v5:
time: 45.1 us; the launch traced here: 44.3 us
  starting transfers between devices  16 us (35%)
  Pallas kernels  15.5 us (34%)
  waiting for transfers between devices  11.7 us (26%)
  local copies, waits for them, and re-layouts  0.86 us (2%)
    pallas_call x1, Pallas kernels, net(): pl.pallas_call(functools.partial(net_kernel, R=R, side=side, halo=halo),...  12.7 us
    all_to_all x1, starting transfers between devices, body(): recv = lax.all_to_all(sent, 'row', split_axis=0, concat_axis=0, tiled=True)  6.35 us
    ppermute x1, waiting for transfers between devices, body(): far = lax.ppermute(own, 'row', beyond)  5.28 us
    ppermute x1, starting transfers between devices, body(): following = lax.ppermute(mine, 'row', beside)  3.34 us
    all_to_all x1, waiting for transfers between devices, body(): recv = lax.all_to_all(sent, 'row', split_axis=0, concat_axis=0, tiled=True)  3.05 us
    ppermute x1, starting transfers between devices, body(): other = lax.ppermute(far, 'row', swap)  2.99 us
    ppermute x1, starting transfers between devices, body(): far = lax.ppermute(own, 'row', beyond)  2.83 us
    pallas_call x2, Pallas kernels, vmem_call(): pl.pallas_call(kernel, out_shape=out_shape, in_specs=[pl.BlockSpec(memory...  2.05 us
  transfers between devices with their start and end apart: 6, of which 5 were waited for; matrix products, arithmetic and copies ran while one was open for 0% of the time, Pallas kernels for 2%

profile of v5, /device:TPU:7, one launch (start us, length us, event | category | flops | bytes accessed | tf_op | source)
XLA Modules:
  0.0 44.3 jit_solution(8629242071514702379)
XLA Ops:
  0.0 0.0 copy-start.2
  0.0 0.8 %copy-done.2 = bf16[64,4,128]{2,1,0:T(4,128)(2,1)S(1)} copy-done((bf16[64,4,128]{2,1,0:T(4,128)(2,1)S(1)}, bf16[64,4,128]{2,1,0:T(4,128)(2,1)}, u32[]{:S(2)}) %copy-start.2) | copy-done | bytes 65560
  0.8 0.0 copy-start.3
  0.8 1.0 %shard_map.73 = bf16[32,32,128]{2,1,0:T(8,128)(2,1)} custom-call(bf16[64,4,128]{2,1,0:T(4,128)(2,1)S(1)} %copy-done.2), custom_call_target="tpu_custom_call" | custom-call | tf_op jit(solution)/shard_map/pallas_call | solution.py:279
  1.8 0.0 copy-start
  1.8 0.0 copy-start.1
  1.8 6.4 %all-to-all-start = ((bf16[32,32,128]{2,1,0:T(8,128)(2,1)}), bf16[32,32,128]{2,1,0:T(8,128)(2,1)S(1)}, u32[]{:S(2)}, u32[]{:S(2)}) async-start(bf16[32,32,128]{2,1,0:T(8,128)(2,1)} %shard_map.73), calls=%async_computation | async-start | bytes 524288 | tf_op jit(solution)/shard_map/all_to_all | solution.py:308
  8.2 0.0 copy-done.3
  8.2 0.5 %collective-permute-start = (bf16[64,4,128]{2,1,0:T(4,128)(2,1)S(1)}, bf16[64,4,128]{2,1,0:T(4,128)(2,1)S(1)}, u32[]{:S(2)}, u32[]{:S(2)}) collective-permute-start(bf16[64,4,128]{2,1,0:T(4,128)(2,1)S(1)} %copy-done.3), channel_id=1, source_target_pairs={{0,1},{1,0},{2,3},{3,2},{4,5},{5,4},{6,7},{7,6},{8,9},{9,8},{10,11... | collective-permute-start | bytes 196616 | tf_op jit(solution)/shard_map/ppermute | solution.py:304
  8.7 0.9 %collective-permute-done = bf16[64,4,128]{2,1,0:T(4,128)(2,1)S(1)} collective-permute-done((bf16[64,4,128]{2,1,0:T(4,128)(2,1)S(1)}, bf16[64,4,128]{2,1,0:T(4,128)(2,1)S(1)}, u32[]{:S(2)}, u32[]{:S(2)}) %collective-permute-start) | collective-permute-done | bytes 65568 | tf_op jit(solution)/shard_map/ppermute | solution.py:304
  9.6 0.0 copy-start.4
  9.6 0.0 copy-start.5
  9.6 0.0 copy-start.6
  9.6 0.0 copy-start.7
  9.6 0.1 pad_maximum_fusion.mine_ref
  9.7 3.3 %collective-permute-start.1 = (bf16[2,64,4,128]{3,2,1,0:T(4,128)(2,1)S(1)}, bf16[2,64,4,128]{3,2,1,0:T(4,128)(2,1)S(1)}, u32[]{:S(2)}, u32[]{:S(2)}) collective-permute-start(bf16[2,64,4,128]{3,2,1,0:T(4,128)(2,1)S(1)} %pad_maximum_fusion.mine_ref), channel_id=1, source_target_pairs={{1,2},{3,4},{5,6},{7,8},{9,10},{11,12},{13,14},{15,16},{17,18},{19... | collective-permute-start | bytes 393224 | tf_op jit(solution)/shard_map/ppermute | solution.py:306
  13.0 0.0 copy-done
  13.0 0.0 copy-done.1
  13.0 0.0 copy-done.4
  13.0 0.0 copy-done.5
  13.1 0.0 copy-done.6
  13.1 0.0 copy-done.7
  13.1 0.8 %prep.1 = (bf16[12,96,192]{2,1,0:T(8,128)(2,1)S(1)}, bf16[8,64,288]{2,1,0:T(8,128)(2,1)S(1)}, f32[8,64,128]{2,1,0:T(8,128)S(1)}, f32[8,32,128]{2,1,0:T(8,128)S(1)}) custom-call(f32[8,64]{1,0:T(8,128)S(1)} %copy-done.4, f32[8,64]{1,0:T(8,128)S(1)} %copy-done.5, bf16[8,32,576]{2,1,0:T(8,128)(2,1)S(1)} %copy-done.1, f32[8,32]{1,0:T(8,128)S(1)} %copy-done.6, ...), custom_call_target="tpu_custom_call" | custom-call | tf_op jit(solution)/shard_map/prep/pallas_call | solution.py:213
  13.9 3.0 %all-to-all-done.recv_ref = bf16[32,32,128]{2,1,0:T(8,128)(2,1)S(1)} async-done(((bf16[32,32,128]{2,1,0:T(8,128)(2,1)}), bf16[32,32,128]{2,1,0:T(8,128)(2,1)S(1)}, u32[]{:S(2)}, u32[]{:S(2)}) %all-to-all-start) | async-done | bytes 262176 | tf_op jit(solution)/shard_map/all_to_all | solution.py:308
  16.9 1.1 %collective-permute-done.1.next_ref = bf16[2,64,4,128]{3,2,1,0:T(4,128)(2,1)S(1)} collective-permute-done((bf16[2,64,4,128]{3,2,1,0:T(4,128)(2,1)S(1)}, bf16[2,64,4,128]{3,2,1,0:T(4,128)(2,1)S(1)}, u32[]{:S(2)}, u32[]{:S(2)}) %collective-permute-start.1) | collective-permute-done | bytes 131104 | tf_op jit(solution)/shard_map/ppermute | solution.py:306
  18.0 1.1 %shard_map.74 = (bf16[16,64,128]{2,1,0:T(8,128)(2,1)S(1)}, bf16[8,64,128]{2,1,0:T(8,128)(2,1)S(1)}) custom-call(bf16[32,32,128]{2,1,0:T(8,128)(2,1)S(1)} %all-to-all-done.recv_ref, bf16[2,64,4,128]{3,2,1,0:T(4,128)(2,1)S(1)} %pad_maximum_fusion.mine_ref, bf16[2,64,4,128]{3,2,1,0:T(4,128)(2,1)S(1)} %collective-permute-done.1.next_ref), custom_call_target="tpu_custom_call" | custom-call | tf_op jit(solution)/shard_map/pallas_call | solution.py:279
  19.1 2.8 %collective-permute-start.2 = (bf16[16,64,128]{2,1,0:T(8,128)(2,1)S(1)}, bf16[16,64,128]{2,1,0:T(8,128)(2,1)S(1)}, u32[]{:S(2)}, u32[]{:S(2)}) collective-permute-start(bf16[16,64,128]{2,1,0:T(8,128)(2,1)S(1)} %get-tuple-element.22.own_ref), channel_id=1, source_target_pairs={{0,4},{2,6},{4,8},{6,10},{8,12},{10,14},{12,16},{14,18},{16,20},{1... | collective-permute-start | bytes 786440 | tf_op jit(solution)/shard_map/ppermute | solution.py:312
  21.9 5.3 %collective-permute-done.2.far_ref = bf16[16,64,128]{2,1,0:T(8,128)(2,1)S(1)} collective-permute-done((bf16[16,64,128]{2,1,0:T(8,128)(2,1)S(1)}, bf16[16,64,128]{2,1,0:T(8,128)(2,1)S(1)}, u32[]{:S(2)}, u32[]{:S(2)}) %collective-permute-start.2) | collective-permute-done | bytes 262176 | tf_op jit(solution)/shard_map/ppermute | solution.py:312
  27.2 3.0 %collective-permute-start.4 = (bf16[16,64,128]{2,1,0:T(8,128)(2,1)S(1)}, bf16[16,64,128]{2,1,0:T(8,128)(2,1)S(1)}, u32[]{:S(2)}, u32[]{:S(2)}) collective-permute-start(bf16[16,64,128]{2,1,0:T(8,128)(2,1)S(1)} %collective-permute-done.2.far_ref), channel_id=1, source_target_pairs={{0,1},{1,0},{2,3},{3,2},{4,5},{5,4},{6,7},{7,6},{8,9},{9,8},{10,11... | collective-permute-start | bytes 786440 | tf_op jit(solution)/shard_map/ppermute | solution.py:314
  30.2 0.0 collective-permute-start.3
  30.2 1.3 %collective-permute-done.3.near_ref = bf16[8,64,128]{2,1,0:T(8,128)(2,1)S(1)} collective-permute-done((bf16[8,64,128]{2,1,0:T(8,128)(2,1)S(1)}, bf16[8,64,128]{2,1,0:T(8,128)(2,1)S(1)}, u32[]{:S(2)}, u32[]{:S(2)}) %collective-permute-start.3) | collective-permute-done | bytes 131104 | tf_op jit(solution)/shard_map/ppermute | solution.py:313
  31.6 0.0 collective-permute-done.4.other_ref
  31.6 12.7 %net.1 = bf16[64,4,128]{2,1,0:T(4,128)(2,1)} custom-call(bf16[16,64,128]{2,1,0:T(8,128)(2,1)S(1)} %get-tuple-element.22.own_ref, bf16[16,64,128]{2,1,0:T(8,128)(2,1)S(1)} %collective-permute-done.2.far_ref, bf16[8,64,128]{2,1,0:T(8,128)(2,1)S(1)} %collective-permute-done.3.near_ref, bf16[16,64,128]{2,1,0:T(8,128)(2,1)S(1)} %collective-permute-done.4.other_ref, ...), custom_call_target="tpu_custom_call" | custom-call | tf_op jit(solution)/shard_map/net/pallas_call | solution.py:168
Async XLA Ops:
  0.0 0.8 %copy-start.2 = (bf16[64,4,128]{2,1,0:T(4,128)(2,1)S(1)}, bf16[64,4,128]{2,1,0:T(4,128)(2,1)}, u32[]{:S(2)}) copy-start(bf16[64,4,128]{2,1,0:T(4,128)(2,1)} %x_ref.1) | copy-start | bytes 196612
  0.8 7.4 %copy-start.3 = (bf16[64,4,128]{2,1,0:T(4,128)(2,1)S(1)}, bf16[64,4,128]{2,1,0:T(4,128)(2,1)}, u32[]{:S(2)}) copy-start(bf16[64,4,128]{2,1,0:T(4,128)(2,1)} %x_ref.1) | copy-start | bytes 196612
  1.8 11.2 %copy-start = (bf16[8,64,288]{2,1,0:T(8,128)(2,1)S(1)}, bf16[8,64,288]{2,1,0:T(8,128)(2,1)}, u32[]{:S(2)}) copy-start(bf16[8,64,288]{2,1,0:T(8,128)(2,1)} %ww_ref.2) | copy-start | bytes 884740
  1.8 11.2 %copy-start.1 = (bf16[8,32,576]{2,1,0:T(8,128)(2,1)S(1)}, bf16[8,32,576]{2,1,0:T(8,128)(2,1)}, u32[]{:S(2)}) copy-start(bf16[8,32,576]{2,1,0:T(8,128)(2,1)} %wn_ref.1) | copy-start | bytes 884740
  1.8 15.1 %all-to-all-start = ((bf16[32,32,128]{2,1,0:T(8,128)(2,1)}), bf16[32,32,128]{2,1,0:T(8,128)(2,1)S(1)}, u32[]{:S(2)}, u32[]{:S(2)}) async-start(bf16[32,32,128]{2,1,0:T(8,128)(2,1)} %shard_map.73), calls=%async_computation | async-start | bytes 524288 | tf_op jit(solution)/shard_map/all_to_all | solution.py:308
  8.2 1.4 %collective-permute-start = (bf16[64,4,128]{2,1,0:T(4,128)(2,1)S(1)}, bf16[64,4,128]{2,1,0:T(4,128)(2,1)S(1)}, u32[]{:S(2)}, u32[]{:S(2)}) collective-permute-start(bf16[64,4,128]{2,1,0:T(4,128)(2,1)S(1)} %copy-done.3), channel_id=1, source_target_pairs={{0,1},{1,0},{2,3},{3,2},{4,5},{5,4},{6,7},{7,6},{8,9},{9,8},{10,11... | collective-permute-start | bytes 196616 | tf_op jit(solution)/shard_map/ppermute | solution.py:304
  9.6 3.5 %copy-start.4 = (f32[8,64]{1,0:T(8,128)S(1)}, f32[8,64]{1,0:T(8,128)}, u32[]{:S(2)}) copy-start(f32[8,64]{1,0:T(8,128)} %go_ref.1) | copy-start | bytes 6148
  9.6 3.5 %copy-start.5 = (f32[8,64]{1,0:T(8,128)S(1)}, f32[8,64]{1,0:T(8,128)}, u32[]{:S(2)}) copy-start(f32[8,64]{1,0:T(8,128)} %bo_ref.1) | copy-start | bytes 6148
  9.6 3.5 %copy-start.6 = (f32[8,32]{1,0:T(8,128)S(1)}, f32[8,32]{1,0:T(8,128)}, u32[]{:S(2)}) copy-start(f32[8,32]{1,0:T(8,128)} %gi_ref.1) | copy-start | bytes 3076
  9.6 3.5 %copy-start.7 = (f32[8,32]{1,0:T(8,128)S(1)}, f32[8,32]{1,0:T(8,128)}, u32[]{:S(2)}) copy-start(f32[8,32]{1,0:T(8,128)} %bi_ref.1) | copy-start | bytes 3076
  9.7 8.4 %collective-permute-start.1 = (bf16[2,64,4,128]{3,2,1,0:T(4,128)(2,1)S(1)}, bf16[2,64,4,128]{3,2,1,0:T(4,128)(2,1)S(1)}, u32[]{:S(2)}, u32[]{:S(2)}) collective-permute-start(bf16[2,64,4,128]{3,2,1,0:T(4,128)(2,1)S(1)} %pad_maximum_fusion.mine_ref), channel_id=1, source_target_pairs={{1,2},{3,4},{5,6},{7,8},{9,10},{11,12},{13,14},{15,16},{17,18},{19... | collective-permute-start | bytes 393224 | tf_op jit(solution)/shard_map/ppermute | solution.py:306
  19.1 8.1 %collective-permute-start.2 = (bf16[16,64,128]{2,1,0:T(8,128)(2,1)S(1)}, bf16[16,64,128]{2,1,0:T(8,128)(2,1)S(1)}, u32[]{:S(2)}, u32[]{:S(2)}) collective-permute-start(bf16[16,64,128]{2,1,0:T(8,128)(2,1)S(1)} %get-tuple-element.22.own_ref), channel_id=1, source_target_pairs={{0,4},{2,6},{4,8},{6,10},{8,12},{10,14},{12,16},{14,18},{16,20},{1... | collective-permute-start | bytes 786440 | tf_op jit(solution)/shard_map/ppermute | solution.py:312
  27.2 4.3 %collective-permute-start.4 = (bf16[16,64,128]{2,1,0:T(8,128)(2,1)S(1)}, bf16[16,64,128]{2,1,0:T(8,128)(2,1)S(1)}, u32[]{:S(2)}, u32[]{:S(2)}) collective-permute-start(bf16[16,64,128]{2,1,0:T(8,128)(2,1)S(1)} %collective-permute-done.2.far_ref), channel_id=1, source_target_pairs={{0,1},{1,0},{2,3},{3,2},{4,5},{5,4},{6,7},{7,6},{8,9},{9,8},{10,11... | collective-permute-start | bytes 786440 | tf_op jit(solution)/shard_map/ppermute | solution.py:314
  30.2 1.3 %collective-permute-start.3 = (bf16[8,64,128]{2,1,0:T(8,128)(2,1)S(1)}, bf16[8,64,128]{2,1,0:T(8,128)(2,1)S(1)}, u32[]{:S(2)}, u32[]{:S(2)}) collective-permute-start(bf16[8,64,128]{2,1,0:T(8,128)(2,1)S(1)} %get-tuple-element.23), channel_id=1, source_target_pairs={{0,1},{1,0},{2,3},{3,2},{4,5},{5,4},{6,7},{7,6},{8,9},{9,8},{10,11... | collective-permute-start | bytes 393224 | tf_op jit(solution)/shard_map/ppermute | solution.py:313
